TPU v7x, 128 devices: a whole 4x4x4 slice. The times are simulated.
128 devices in a mesh: lon: 16 (over z, y_lo, core), lat: 8 (over x, y_hi).
Axes of the slice: x: 4, y: 4 (y_hi: 2, y_lo: 2; y = y_hi * 2 + y_lo), z: 4, core: 2. Of those that a mesh axis runs over, the one named last changes fastest.
Arguments:
- state: float32 [168, 128, 2048], P(None, 'lat', 'lon'), may hold values from -6 to 6
- noise: float32 [168, 128, 2048], P(None, 'lat', 'lon'), may hold values from -6 to 6
- first_kernel: bfloat16 [9, 256, 168], replicated, may hold values from -0.15625 to 0.15625
- middle_kernels: bfloat16 [2, 9, 256, 256], replicated, may hold values from -0.21875 to 0.21875
- last_kernel: bfloat16 [9, 168, 256], replicated, may hold values from -0.21875 to 0.21875
- obs_values: bfloat16 [12288, 22, 128], P(('lon', 'lat')), may hold values from -6 to 6
- obs_holder: int32 [12288, 1], P(('lon', 'lat')), may hold values from 0 to 127; in each aligned block of 96 rows (0 to 95, 96 to 191, ...) at most 2 rows name the same one
- obs_tile: int32 [12288], P(('lon', 'lat')), may hold values from 0 to 15
- obs_operator: bfloat16 [22, 168], replicated, may hold values from -0.5 to 0.5
- obs_precision: float32 [22], replicated, may hold values from 0.3 to 3
- noise_level: float32 [1], replicated, may hold values from 0.25 to 1
- step_size: float32 [1], replicated, may hold values from 0.05 to 0.2
Outputs:
- state_next: float32 [168, 128, 2048], P(None, 'lat', 'lon')
Inputs may be any that keep to these rules, and one draw needn't show every extreme that they name: `obs_holder`: the holder index counts lon-major: lon index times 8 plus lat index; the 96 blocks that one device holds (an aligned block of rows) name one holder at most 2 times, and exactly that often for some holder in every draw.
All inputs are finite; a program needn't handle non-finite values.
Results may differ from a plain program's by a relative error of at most 0.0095.
Values may be sent and summed in bfloat16 or wider, within the bound.
No kernel may reach another device: no remote copies, remote signals or barrier semaphores. Data moves between devices by JAX's collectives and lax.ppermute only.
A program may use at most 128 MiB of HBM per device.

v0:
```python
import jax
import jax.numpy as jnp
from jax import lax
from jax.experimental import pallas as pl
from jax.experimental.pallas import tpu as pltpu
from jax.sharding import PartitionSpec as P

LAYERS = 4
CAPACITY = 2
HALO = 4
SIDE = 8
LANES = 256
SLOT = 24
BLOCK = 4
F32 = jnp.float32
BF16 = jnp.bfloat16


def vmem_specs(count):
    return [pl.BlockSpec(memory_space=pltpu.VMEM) for _ in range(count)]


def smem_spec():
    return pl.BlockSpec(memory_space=pltpu.SMEM)


def params():
    return pltpu.CompilerParams(vmem_limit_bytes=60 << 20)


def pack_kernel(slot_ref, tile_ref, values_ref, out_ref, wide_ref):
    channels, count, width = values_ref.shape
    slots = out_ref.shape[0] // SLOT
    onehot = lax.broadcasted_iota(jnp.int32, (slots, count), 0) == slot_ref[...]
    onehot = onehot.astype(F32).astype(BF16)
    for k in range(channels):
        wide_ref[pl.ds(k, slots, stride=SLOT), :] = jnp.dot(
            onehot, values_ref[k], preferred_element_type=F32
        )
    numbers = jnp.broadcast_to((tile_ref[...] + 1).astype(F32), (count, width)).astype(BF16)
    placed = jnp.dot(onehot, numbers, preferred_element_type=F32)
    for k in range(channels, SLOT):
        wide_ref[pl.ds(k, slots, stride=SLOT), :] = placed
    out_ref[...] = wide_ref[...].astype(BF16)


def pack_blocks(slots, tiles, values, slot_count):
    width = values.shape[2]
    return pl.pallas_call(
        pack_kernel,
        out_shape=jax.ShapeDtypeStruct((slot_count * SLOT, width), BF16),
        in_specs=vmem_specs(3),
        out_specs=vmem_specs(1)[0],
        scratch_shapes=[pltpu.VMEM((slot_count * SLOT, width), F32)],
        compiler_params=params(),
        name="pack_blocks",
    )(slots[None, :], tiles[:, None], jnp.transpose(values, (1, 0, 2)))


def put_shifted(dst_ref, row, width, act):
    size = act.shape[0]
    at = pl.ds(row * width, size)
    dst_ref[at, LANES : 2 * LANES] = act.astype(BF16)
    dst_ref[at, 0:LANES] = pltpu.roll(act, 1, 0).astype(BF16)
    dst_ref[at, 2 * LANES : 3 * LANES] = pltpu.roll(act, size - 1, 0).astype(BF16)


def conv_block(src_ref, row, rows, width, w_ref, flip):
    acc = None
    for p in range(3):
        wide = src_ref[pl.ds((row + p) * width, rows * width), :]
        for q in range(3):
            tap = 3 * p + q
            part = jnp.dot(
                wide[:, q * LANES : (q + 1) * LANES],
                w_ref[8 - tap if flip else tap],
                preferred_element_type=F32,
            )
            acc = part if acc is None else acc + part
    return acc


def conv_layer(rows, compute, finish, acc_a, acc_b):
    full, rest = divmod(rows, BLOCK)
    acc_a[...] = compute(0, BLOCK)
    pairs = (full - 1) // 2

    def body(j, carry):
        row = 2 * BLOCK * j
        acc_b[...] = compute(row + BLOCK, BLOCK)
        finish(row, BLOCK, acc_a[...])
        acc_a[...] = compute(row + 2 * BLOCK, BLOCK)
        finish(row + BLOCK, BLOCK, acc_b[...])
        return carry

    lax.fori_loop(0, pairs, body, 0)
    done = 2 * pairs
    if full - 1 > done:
        acc_b[...] = compute((done + 1) * BLOCK, BLOCK)
        finish(done * BLOCK, BLOCK, acc_a[...])
        last = (full - 1, acc_b)
        free = acc_a
    else:
        last = (full - 1, acc_a)
        free = acc_b
    if rest:
        tail = compute(full * BLOCK, rest)
        size = tail.shape[0]
        free[0:size, :] = tail
        finish(last[0] * BLOCK, BLOCK, last[1][...])
        finish(full * BLOCK, rest, free[0:size, :])
    else:
        finish(last[0] * BLOCK, BLOCK, last[1][...])


def forward_kernel(
    band_ref, x_ref, w0, w1, w2, w3, op_ref, pre_ref, pred_ref, d0, d1, d2, buf_a, buf_b, acc_a, acc_b
):
    rows = pre_ref.shape[0]
    width = pre_ref.shape[1]
    cells = width - 2 * SIDE
    weights = (w0, w1, w2, w3)
    slopes = (d0, d1, d2)

    def fill(i, carry):
        part = x_ref[pl.ds(i * 2 * width, 2 * width), :]
        put_shifted(buf_a, i * 2, width, part.astype(F32))
        return carry

    lax.fori_loop(0, (rows + 2 * HALO) // 2, fill, 0)
    src, dst = buf_a, buf_b
    for layer in range(LAYERS):
        margin = HALO - 1 - layer
        count = rows + 2 * margin

        def compute(row, n, src=src, layer=layer):
            return conv_block(src, row, n, width, weights[layer], False)

        if layer < LAYERS - 1:

            def finish(row, n, value, dst=dst, layer=layer):
                gate = 0.5 + 0.5 * jnp.tanh(0.5 * value)
                act = value * gate
                slope = gate + act * (1.0 - gate)
                slopes[layer][pl.ds(row * width, n * width), :] = slope.astype(BF16)
                put_shifted(dst, row, width, act)

        else:

            def finish(row, n, value):
                for i in range(n):
                    part = value[i * width : (i + 1) * width, :]
                    pre_ref[row + i] = part
                    own = x_ref[pl.ds((row + i + HALO) * width, width), :]
                    clean = (own.astype(F32) + part)[SIDE : SIDE + cells, :].astype(BF16)
                    pred_ref[row + i] = lax.dot_general(
                        op_ref[...], clean, (((1,), (1,)), ((), ())), preferred_element_type=F32
                    )

        conv_layer(count, compute, finish, acc_a, acc_b)
        if layer < LAYERS - 1:
            size = margin * width

            def clear(first, dst=dst, layer=layer, size=size):
                slopes[layer][first : first + size, :] = jnp.zeros((size, LANES), BF16)
                dst[first : first + size, :] = jnp.zeros((size, 3 * LANES), BF16)

            @pl.when(band_ref[0] == 0)
            def _():
                clear(0)

            @pl.when(band_ref[0] == band_ref[1] - 1)
            def _(count=count, size=size):
                clear(count * width - size)

        src, dst = dst, src


def forward_pass(band, x, weights, operator, rows, width):
    slope_rows = [rows + 2 * (HALO - 1 - layer) for layer in range(LAYERS - 1)]
    padded = (rows + 2 * HALO) * width
    return pl.pallas_call(
        forward_kernel,
        out_shape=(
            jax.ShapeDtypeStruct((rows, width, LANES), F32),
            jax.ShapeDtypeStruct((rows, operator.shape[0], width - 2 * SIDE), F32),
        )
        + tuple(jax.ShapeDtypeStruct((n * width, LANES), BF16) for n in slope_rows),
        in_specs=[smem_spec()] + vmem_specs(6),
        out_specs=tuple(vmem_specs(5)),
        scratch_shapes=[pltpu.VMEM((padded, 3 * LANES), BF16)] * 2
        + [pltpu.VMEM((BLOCK * width, LANES), F32)] * 2,
        compiler_params=params(),
        name="forward_pass",
    )(band, x, *weights, operator)


def backward_kernel(
    scale_ref, recv_ref, pred_ref, pre_ref, d0, d1, d2, op_ref, prec_ref, w0, w1, w2, w3,
    own_ref, top_ref, bot_ref, wide_ref, sums_ref, buf_a, buf_b, acc_a, acc_b,
):
    rows, width = pre_ref.shape[0], pre_ref.shape[1]
    cells = width - 2 * SIDE
    channels = 22
    slots = recv_ref.shape[0] // SLOT
    lead = HALO + 1
    weights = (w0, w1, w2, w3)
    slopes = (d0, d1, d2)
    zeros = jnp.zeros((4 * width, 3 * LANES), BF16)
    buf_a[width : 5 * width, :] = zeros
    buf_a[(rows + 5) * width : (rows + 9) * width, :] = zeros
    buf_b[0 : 4 * width, :] = zeros
    buf_b[(rows + 6) * width : (rows + 10) * width, :] = zeros

    wide_ref[...] = recv_ref[...].astype(F32)
    sums_ref[...] = jnp.zeros(sums_ref.shape, F32)
    numbers = wide_ref[pl.ds(channels, slots, stride=SLOT), :]
    lane = lax.broadcasted_iota(jnp.int32, (slots, cells), 1).astype(F32) + 1.0
    onehot = jnp.transpose((numbers == lane).astype(F32))[0:rows, :].astype(BF16)
    held = jnp.dot(onehot, jnp.ones((slots, cells), BF16), preferred_element_type=F32)
    for k in range(channels):
        part = wide_ref[pl.ds(k, slots, stride=SLOT), :].astype(BF16)
        sums_ref[pl.ds(k, rows, stride=32), :] = jnp.dot(onehot, part, preferred_element_type=F32)
    for r in range(rows):
        summed = sums_ref[r * 32 : (r + 1) * 32, :]
        weighted = (summed - held[r : r + 1, :] * pred_ref[r]) * prec_ref[...]
        pulled = jnp.dot(
            jnp.transpose(weighted).astype(BF16), op_ref[...], preferred_element_type=F32
        )
        side = jnp.zeros((SIDE, LANES), F32)
        start = pre_ref[r][SIDE : SIDE + cells, :] * scale_ref[0] + pulled
        own_ref[r] = jnp.concatenate([side, start, side], axis=0)
        put_shifted(buf_a, r + lead, width, jnp.concatenate([side, pulled, side], axis=0))

    src, dst = buf_a, buf_b
    for layer in range(LAYERS - 1, -1, -1):
        margin = LAYERS - layer
        count = rows + 2 * margin

        def compute(row, n, src=src, layer=layer, margin=margin):
            return conv_block(src, row + lead - margin - 1, n, width, weights[layer], True)

        if layer > 0:

            def finish(row, n, value, dst=dst, layer=layer, margin=margin):
                slope = slopes[layer - 1][pl.ds(row * width, n * width), :]
                put_shifted(dst, row + lead - margin, width, value * slope.astype(F32))

            conv_layer(count, compute, finish, acc_a, acc_b)
        else:
            top_ref[...] = compute(0, HALO).astype(BF16)
            bot_ref[...] = compute(rows + HALO, HALO).astype(BF16)

            def inner(row, n, src=src, layer=layer, margin=margin):
                return compute(row + HALO, n)

            def finish(row, n, value):
                for i in range(n):
                    own_ref[row + i] = own_ref[row + i] + value[i * width : (i + 1) * width, :]

            conv_layer(rows, inner, finish, acc_a, acc_b)
        src, dst = dst, src


def backward_pass(scale, recv, pred, pre, slopes, operator, precision, weights):
    rows, width = pre.shape[0], pre.shape[1]
    padded = (rows + 2 * (HALO + 1)) * width
    return pl.pallas_call(
        backward_kernel,
        out_shape=(
            jax.ShapeDtypeStruct((rows, width, LANES), F32),
            jax.ShapeDtypeStruct((HALO * width, LANES), BF16),
            jax.ShapeDtypeStruct((HALO * width, LANES), BF16),
        ),
        in_specs=[smem_spec()] + vmem_specs(12),
        out_specs=tuple(vmem_specs(3)),
        scratch_shapes=[
            pltpu.VMEM(recv.shape, F32),
            pltpu.VMEM((rows * 32, recv.shape[1]), F32),
        ]
        + [pltpu.VMEM((padded, 3 * LANES), BF16)] * 2
        + [pltpu.VMEM((BLOCK * width, LANES), F32)] * 2,
        compiler_params=params(),
        name="backward_pass",
    )(scale, recv, pred, pre, *slopes, operator, precision, *weights)


def final_kernel(
    scale_ref, own_ref, above_ref, below_ref, left_ref, right_ref, state_ref, noise_ref, out_ref
):
    rows, width = own_ref.shape[0], own_ref.shape[1]
    cells = width - 2 * SIDE
    channels = state_ref.shape[0]
    for r in range(rows):
        total = own_ref[r][SIDE : SIDE + cells, :]
        if r < HALO:
            total = total + above_ref[r * width : (r + 1) * width, :].astype(F32)[SIDE : SIDE + cells, :]
        if r >= rows - HALO:
            at = r - (rows - HALO)
            total = total + below_ref[at * width : (at + 1) * width, :].astype(F32)[SIDE : SIDE + cells, :]
        first = total[0:SIDE, :] + left_ref[r]
        last = total[cells - SIDE : cells, :] + right_ref[r]
        total = jnp.concatenate([first, total[SIDE : cells - SIDE, :], last], axis=0)
        turned = jnp.transpose(total)[0:channels, :]
        out_ref[:, r, :] = (
            state_ref[:, r, :] + scale_ref[0] * turned + scale_ref[1] * noise_ref[:, r, :]
        )


def final_pass(scale, own, above, below, left, right, state, noise):
    return pl.pallas_call(
        final_kernel,
        out_shape=jax.ShapeDtypeStruct(state.shape, F32),
        in_specs=[smem_spec()] + vmem_specs(7),
        out_specs=vmem_specs(1)[0],
        compiler_params=params(),
        name="final_pass",
    )(scale, own, above, below, left, right, state, noise)


def swap_pairs(size, first, wrap):
    pairs = []
    for low in range(first, size if wrap else size - 1, 2):
        high = (low + 1) % size
        pairs += [(low, high), (high, low)]
    return pairs


def exchange(axis, wrap, to_before, to_after):
    size = lax.axis_size(axis)
    even = lax.axis_index(axis) % 2 == 0
    near = lax.ppermute(jnp.where(even, to_after, to_before), axis, swap_pairs(size, 0, wrap))
    far = lax.ppermute(jnp.where(even, to_before, to_after), axis, swap_pairs(size, 1, wrap))
    return jnp.where(even, far, near), jnp.where(even, near, far)


def pad_to(values, shape):
    return jnp.pad(values, [(0, n - m) for m, n in zip(values.shape, shape)])


def shards(
    state,
    noise,
    first_kernel,
    middle_kernels,
    last_kernel,
    obs_values,
    obs_holder,
    obs_tile,
    obs_operator,
    obs_precision,
    noise_level,
    step_size,
):
    channels, rows, cells = state.shape
    width = cells + 2 * SIDE
    square = (9, LANES, LANES)
    kernels = [pad_to(first_kernel, square), middle_kernels[0], middle_kernels[1], pad_to(last_kernel, square)]
    turned = [jnp.transpose(kernel, (0, 2, 1)) for kernel in kernels]

    targets = obs_holder[:, 0]
    count = targets.shape[0]
    positions = lax.broadcasted_iota(jnp.int32, (count, count), 0)
    earlier = lax.broadcasted_iota(jnp.int32, (count, count), 1)
    before = (targets[:, None] == targets[None, :]) & (earlier < positions)
    slots = targets * CAPACITY + jnp.sum(before.astype(jnp.int32), axis=1)
    holders = lax.axis_size(("lon", "lat"))
    packed = pack_blocks(slots, obs_tile, obs_values, holders * CAPACITY)
    recv = lax.all_to_all(
        packed.reshape(holders, CAPACITY * SLOT, cells), ("lon", "lat"), split_axis=0, concat_axis=0, tiled=True
    ).reshape(packed.shape)

    x = jnp.transpose(state.astype(BF16), (1, 2, 0))
    x = pad_to(x, (rows, cells, LANES))
    left, right = exchange("lon", True, x[:, :SIDE], x[:, cells - SIDE :])
    x = jnp.concatenate([left, x, right], axis=1)
    above, below = exchange("lat", False, x[:HALO], x[rows - HALO :])
    x = jnp.concatenate([above, x, below], axis=0).reshape(-1, LANES)

    band = jnp.stack([lax.axis_index("lat"), lax.axis_size("lat")]).astype(jnp.int32)
    operator = pad_to(obs_operator, (32, LANES))
    precision = pad_to(obs_precision[:, None], (32, 1))
    pre, pred, *slopes = forward_pass(band, x, turned, operator, rows, width)
    inverse = (1.0 / (noise_level * noise_level)).astype(F32)
    own, top, bottom = backward_pass(inverse, recv, pred, pre, slopes, operator, precision, kernels)
    above, below = exchange("lat", False, top, bottom)
    above_side = above.reshape(HALO, width, LANES)
    below_side = below.reshape(HALO, width, LANES)

    def edge(at):
        added = [
            above_side[:, at : at + SIDE].astype(F32),
            jnp.zeros((rows - 2 * HALO, SIDE, LANES), F32),
            below_side[:, at : at + SIDE].astype(F32),
        ]
        return (own[:, at : at + SIDE] + jnp.concatenate(added, axis=0)).astype(BF16)

    left, right = exchange("lon", True, edge(0), edge(width - SIDE))
    scale = jnp.stack([step_size[0], jnp.sqrt(2.0 * step_size[0])])
    return final_pass(scale, own, above, below, left.astype(F32), right.astype(F32), state, noise)


def solution(mesh):
    placed = (
        P(None, "lat", "lon"),
        P(None, "lat", "lon"),
        P(),
        P(),
        P(),
        P(("lon", "lat"), None, None),
        P(("lon", "lat"), None),
        P(("lon", "lat")),
        P(),
        P(),
        P(),
        P(),
    )
    return jax.shard_map(
        shards, mesh=mesh, in_specs=placed, out_specs=P(None, "lat", "lon"), check_vma=False
    )
```

profile of v0, /device:TPU:2, one launch (start us, length us, event | category | flops | bytes accessed | tf_op | source)
XLA Modules:
  0.0 137.7 jit_solution(12989353897345544434)
XLA Ops:
  0.0 1.4 %convert_element_type.41 = bf16[168,16,128]{2,1,0:T(8,128)(2,1)S(1)} convert(f32[168,16,128]{2,1,0:T(8,128)} %state_ref.1) | non-fusion elementwise | flops 344064 | bytes 2064384 | tf_op jit(solution)/shard_map/convert_element_type | solution.py:373
  2.2 4.6 %collective-permute-start = (bf16[16,8,256]{2,1,0:T(8,128)(2,1)S(1)}, bf16[16,8,256]{2,1,0:T(8,128)(2,1)S(1)}, u32[]{:S(2)}, u32[]{:S(2)}) collective-permute-start(bf16[16,8,256]{2,1,0:T(8,128)(2,1)S(1)} %get-tuple-element.33), channel_id=1, source_target_pairs={{8,16},{16,8},{24,32},{32,24},{40,48},{48,40},{56,64},{64,56},{72,... | collective-permute-start | bytes 196616 | tf_op jit(solution)/shard_map/ppermute | solution.py:333
  6.7 0.7 copy.29.tile_ref
  8.2 3.2 %pack_blocks.1 = bf16[6144,128]{1,0:T(8,128)(2,1)} custom-call(s32[1,96]{1,0:T(1,128)} %bitcast_add_fusion.slot_ref, s32[96,1]{1,0:T(8,128)} %copy.29.tile_ref, bf16[22,96,128]{2,1,0:T(8,128)(2,1)} %bitcast.35), custom_call_target="tpu_custom_call" | custom-call | tf_op jit(solution)/shard_map/pack_blocks/pallas_call | solution.py:49
  11.3 8.0 %all-to-all-start = ((bf16[128,48,128]{2,1,0:T(8,128)(2,1)}), bf16[128,48,128]{2,1,0:T(8,128)(2,1)}, u32[]{:S(2)}, u32[]{:S(2)}) async-start(bf16[128,48,128]{2,1,0:T(8,128)(2,1)} %bitcast.32), calls=%async_computation | async-start | bytes 3145728 | tf_op jit(solution)/shard_map/all_to_all | solution.py:369
  19.4 3.8 %slice_bitcast_fusion.1 = (bf16[9,256,256]{2,1,0:T(8,128)(2,1)}, bf16[9,256,256]{1,2,0:T(8,128)(2,1)}, bf16[9,256,256]{1,2,0:T(8,128)(2,1)S(1)}, bf16[9,256,256]{2,1,0:T(8,128)(2,1)}) fusion(bf16[2,9,256,256]{3,2,1,0:T(8,128)(2,1)} %param.15), kind=kLoop, calls=%fused_computation.2 | loop fusion | bytes 7077888 | tf_op jit(solution)/shard_map/squeeze | solution.py:358
  23.4 2.3 %copy.31 = bf16[9,256,168]{2,1,0:T(8,128)(2,1)} copy(bf16[9,256,168]{1,2,0:T(8,128)(2,1)} %param.14) | data formatting | bytes 1548288 | tf_op args[2]
  26.3 0.9 broadcast_select_fusion.11
  27.2 0.9 broadcast_select_fusion.7
  28.1 0.8 broadcast_select_fusion.6
  28.8 3.0 %collective-permute-start.3 = (bf16[4,144,256]{2,1,0:T(8,128)(2,1)}, bf16[4,144,256]{2,1,0:T(8,128)(2,1)}, u32[]{:S(2)}, u32[]{:S(2)}) collective-permute-start(bf16[4,144,256]{2,1,0:T(8,128)(2,1)} %broadcast_select_fusion.6), channel_id=1, source_target_pairs={{0,1},{1,0},{2,3},{3,2},{4,5},{5,4},{6,7},{7,6},{8,9},{9,8},{10,11... | collective-permute-start | bytes 884744 | tf_op jit(solution)/shard_map/ppermute | solution.py:332
  31.8 3.0 %collective-permute-start.2 = (bf16[4,144,256]{2,1,0:T(8,128)(2,1)}, bf16[4,144,256]{2,1,0:T(8,128)(2,1)}, u32[]{:S(2)}, u32[]{:S(2)}) collective-permute-start(bf16[4,144,256]{2,1,0:T(8,128)(2,1)} %get-tuple-element.24), channel_id=1, source_target_pairs={{1,2},{2,1},{3,4},{4,3},{5,6},{6,5},{9,10},{10,9},{11,12},{12,11},... | collective-permute-start | bytes 884744 | tf_op jit(solution)/shard_map/ppermute | solution.py:333
  34.9 2.0 %fusion.5 = (bf16[9,256,256]{2,1,0:T(8,128)(2,1)}, bf16[9,256,256]{1,2,0:T(8,128)(2,1)S(1)}, bf16[9,256,256]{1,2,0:T(8,128)(2,1)}, bf16[9,256,256]{2,1,0:T(8,128)(2,1)}) fusion(bf16[9,256,168]{2,1,0:T(8,128)(2,1)S(1)} %copy-done.1, bf16[9,168,256]{2,1,0:T(8,128)(2,1)S(1)} %copy-done.4), kind=kLoop, calls=%fused_computation.40 | loop fusion | bytes 6266880 | tf_op jit(solution)/shard_map/jit(_pad)/pad | solution.py:338
  36.9 1.6 %copy.32.w0 = bf16[9,256,256]{2,1,0:T(8,128)(2,1)} copy(bf16[9,256,256]{1,2,0:T(8,128)(2,1)S(1)} %get-tuple-element.32) | data formatting | bytes 2359296 | tf_op jit(solution)/shard_map/transpose | solution.py:359
  38.5 2.5 %copy.35.w3 = bf16[9,256,256]{2,1,0:T(8,128)(2,1)} copy(bf16[9,256,256]{1,2,0:T(8,128)(2,1)} %get-tuple-element.51) | data formatting | bytes 2359296 | tf_op jit(solution)/shard_map/transpose | solution.py:359
  41.0 1.5 %copy.33.w1 = bf16[9,256,256]{2,1,0:T(8,128)(2,1)} copy(bf16[9,256,256]{1,2,0:T(8,128)(2,1)S(1)} %copy-done) | data formatting | bytes 2359296 | tf_op jit(solution)/shard_map/transpose | solution.py:359
  42.6 1.6 %copy.34.w2 = bf16[9,256,256]{2,1,0:T(8,128)(2,1)} copy(bf16[9,256,256]{1,2,0:T(8,128)(2,1)S(1)} %get-tuple-element.29) | data formatting | bytes 2359296 | tf_op jit(solution)/shard_map/transpose | solution.py:359
  46.8 5.0 %collective-permute-done.3 = bf16[4,144,256]{2,1,0:T(8,128)(2,1)} collective-permute-done((bf16[4,144,256]{2,1,0:T(8,128)(2,1)}, bf16[4,144,256]{2,1,0:T(8,128)(2,1)}, u32[]{:S(2)}, u32[]{:S(2)}) %collective-permute-start.3) | collective-permute-done | bytes 294944 | tf_op jit(solution)/shard_map/ppermute | solution.py:332
  51.8 1.1 broadcast_select_fusion.5
  52.9 1.4 %pad_maximum_fusion = bf16[24,144,256]{2,1,0:T(8,128)(2,1)} fusion(bf16[4,144,256]{2,1,0:T(8,128)(2,1)S(1)} %get-tuple-element.42, bf16[16,8,256]{2,1,0:T(8,128)(2,1)S(1)} %get-tuple-element.50, bf16[16,128,256]{2,1,0:T(8,128)(2,1)S(1)} %pad.20, bf16[16,8,256]{2,1,0:T(8,128)(2,1)S(1)} %get-tuple-element.49, bf16[4,144,256]{2,1,0:T(8,128)(2,1)S(1)} %get-tuple-element.41), kind=kLoop, calls=%fused_computation | loop fusion | flops 8847360 | bytes 3538944 | tf_op jit(solution)/shard_map/concatenate | solution.py:378
  54.3 24.3 %forward_pass.1 = (f32[16,144,256]{2,1,0:T(8,128)}, f32[16,32,128]{2,1,0:T(8,128)}, bf16[3168,256]{1,0:T(8,128)(2,1)}, bf16[2880,256]{1,0:T(8,128)(2,1)}, bf16[2592,256]{1,0:T(8,128)(2,1)}) custom-call(s32[2]{0:T(128)} %pad_add_fusion.band_ref, bf16[3456,256]{1,0:T(8,128)(2,1)} %bitcast.31, bf16[9,256,256]{2,1,0:T(8,128)(2,1)} %copy.32.w0, ...), custom_call_target="tpu_custom_call" | custom-call | tf_op jit(solution)/shard_map/forward_pass/pallas_call | solution.py:182
  78.7 24.5 %backward_pass.1 = (f32[16,144,256]{2,1,0:T(8,128)}, bf16[576,256]{1,0:T(8,128)(2,1)}, bf16[576,256]{1,0:T(8,128)(2,1)}) custom-call(f32[1]{0:T(128)S(6)} %div.3.scale_ref, bf16[6144,128]{1,0:T(8,128)(2,1)} %bitcast.6.recv_ref, f32[16,32,128]{2,1,0:T(8,128)} %get-tuple-element.13.pred_ref, f32[16,144,256]{2,1,0:T(8,128)} %get-tuple-element.14.pre_ref, ...), custom_call_target="tpu_custom_call" | custom-call | tf_op jit(solution)/shard_map/backward_pass/pallas_call | solution.py:268
  103.1 1.1 broadcast_select_fusion.2
  104.2 2.9 %collective-permute-start.4 = (bf16[576,256]{1,0:T(8,128)(2,1)S(1)}, bf16[576,256]{1,0:T(8,128)(2,1)S(1)}, u32[]{:S(2)}, u32[]{:S(2)}) collective-permute-start(bf16[576,256]{1,0:T(8,128)(2,1)S(1)} %get-tuple-element.40), channel_id=1, source_target_pairs={{1,2},{2,1},{3,4},{4,3},{5,6},{6,5},{9,10},{10,9},{11,12},{12,11},... | collective-permute-start | bytes 884744 | tf_op jit(solution)/shard_map/ppermute | solution.py:333
  107.1 3.6 %collective-permute-start.5 = (bf16[576,256]{1,0:T(8,128)(2,1)S(1)}, bf16[576,256]{1,0:T(8,128)(2,1)S(1)}, u32[]{:S(2)}, u32[]{:S(2)}) collective-permute-start(bf16[576,256]{1,0:T(8,128)(2,1)S(1)} %get-tuple-element.39), channel_id=1, source_target_pairs={{0,1},{1,0},{2,3},{3,2},{4,5},{5,4},{6,7},{7,6},{8,9},{9,8},{10,11... | collective-permute-start | bytes 884744 | tf_op jit(solution)/shard_map/ppermute | solution.py:332
  111.4 5.8 %collective-permute-done.4 = bf16[576,256]{1,0:T(8,128)(2,1)S(1)} collective-permute-done((bf16[576,256]{1,0:T(8,128)(2,1)S(1)}, bf16[576,256]{1,0:T(8,128)(2,1)S(1)}, u32[]{:S(2)}, u32[]{:S(2)}) %collective-permute-start.4) | collective-permute-done | bytes 294944 | tf_op jit(solution)/shard_map/ppermute | solution.py:333
  117.2 6.2 %collective-permute-done.5 = bf16[576,256]{1,0:T(8,128)(2,1)S(1)} collective-permute-done((bf16[576,256]{1,0:T(8,128)(2,1)S(1)}, bf16[576,256]{1,0:T(8,128)(2,1)S(1)}, u32[]{:S(2)}, u32[]{:S(2)}) %collective-permute-start.5) | collective-permute-done | bytes 294944 | tf_op jit(solution)/shard_map/ppermute | solution.py:332
  123.5 1.2 broadcast_select_fusion.8
  124.8 3.3 %collective-permute-start.6 = (bf16[16,8,256]{2,1,0:T(8,128)(2,1)S(1)}, bf16[16,8,256]{2,1,0:T(8,128)(2,1)S(1)}, u32[]{:S(2)}, u32[]{:S(2)}) collective-permute-start(bf16[16,8,256]{2,1,0:T(8,128)(2,1)S(1)} %broadcast_select_fusion.9), channel_id=1, source_target_pairs={{8,16},{16,8},{24,32},{32,24},{40,48},{48,40},{56,64},{64,56},{72,... | collective-permute-start | bytes 196616 | tf_op jit(solution)/shard_map/ppermute | solution.py:333
  128.6 2.0 %collective-permute-done.6 = bf16[16,8,256]{2,1,0:T(8,128)(2,1)S(1)} collective-permute-done((bf16[16,8,256]{2,1,0:T(8,128)(2,1)S(1)}, bf16[16,8,256]{2,1,0:T(8,128)(2,1)S(1)}, u32[]{:S(2)}, u32[]{:S(2)}) %collective-permute-start.6) | collective-permute-done | bytes 65568 | tf_op jit(solution)/shard_map/ppermute | solution.py:333
  130.7 0.7 select_convert_fusion
  131.4 6.3 %final_pass.1 = f32[168,16,128]{2,1,0:T(8,128)} custom-call(f32[2]{0:T(128)} %pad_maximum_fusion.4.scale_ref, f32[16,144,256]{2,1,0:T(8,128)} %get-tuple-element.18.own_ref, bf16[576,256]{1,0:T(8,128)(2,1)} %copy-done.3, bf16[576,256]{1,0:T(8,128)(2,1)} %copy-done.2, f32[16,8,256]{2,1,0:T(8,128)} %get-tuple-element.48.left_ref, ...), custom_call_target="tpu_custom_call" | custom-call | tf_op jit(solution)/shard_map/final_pass/pallas_call | solution.py:311
  (43 shorter events, 5.0 us)
Async XLA Ops:
  1.4 5.3 %copy-start.7 = (s32[96]{0:T(128)S(1)}, s32[96]{0:T(128)}, u32[]{:S(2)}) copy-start(s32[96]{0:T(128)} %param.19) | copy-start | bytes 1156
  1.4 6.0 %copy-start.9 = (s32[96,1]{0,1:T(1,128)S(1)}, s32[96,1]{0,1:T(1,128)}, u32[]{:S(2)}) copy-start(s32[96,1]{0,1:T(1,128)} %param.18) | copy-start | bytes 1156
  2.2 23.5 %collective-permute-start = (bf16[16,8,256]{2,1,0:T(8,128)(2,1)S(1)}, bf16[16,8,256]{2,1,0:T(8,128)(2,1)S(1)}, u32[]{:S(2)}, u32[]{:S(2)}) collective-permute-start(bf16[16,8,256]{2,1,0:T(8,128)(2,1)S(1)} %get-tuple-element.33), channel_id=1, source_target_pairs={{8,16},{16,8},{24,32},{32,24},{40,48},{48,40},{56,64},{64,56},{72,... | collective-permute-start | bytes 196616 | tf_op jit(solution)/shard_map/ppermute | solution.py:333
  6.7 19.6 %collective-permute-start.1 = (bf16[16,8,256]{2,1,0:T(8,128)(2,1)S(1)}, bf16[16,8,256]{2,1,0:T(8,128)(2,1)}, u32[]{:S(2)}, u32[]{:S(2)}) collective-permute-start(bf16[16,8,256]{2,1,0:T(8,128)(2,1)S(1)} %get-tuple-element.34), channel_id=1, source_target_pairs={{0,8},{8,0},{16,24},{24,16},{32,40},{40,32},{48,56},{56,48},{64,72... | collective-permute-start | bytes 196616 | tf_op jit(solution)/shard_map/ppermute | solution.py:332
  11.3 67.3 %all-to-all-start = ((bf16[128,48,128]{2,1,0:T(8,128)(2,1)}), bf16[128,48,128]{2,1,0:T(8,128)(2,1)}, u32[]{:S(2)}, u32[]{:S(2)}) async-start(bf16[128,48,128]{2,1,0:T(8,128)(2,1)} %bitcast.32), calls=%async_computation | async-start | bytes 3145728 | tf_op jit(solution)/shard_map/all_to_all | solution.py:369
  25.7 9.2 %copy-start.1 = (bf16[9,256,168]{2,1,0:T(8,128)(2,1)S(1)}, bf16[9,256,168]{2,1,0:T(8,128)(2,1)}, u32[]{:S(2)}) copy-start(bf16[9,256,168]{2,1,0:T(8,128)(2,1)} %copy.31) | copy-start | bytes 2322436
  25.7 9.2 %copy-start.4 = (bf16[9,168,256]{2,1,0:T(8,128)(2,1)S(1)}, bf16[9,168,256]{2,1,0:T(8,128)(2,1)}, u32[]{:S(2)}) copy-start(bf16[9,168,256]{2,1,0:T(8,128)(2,1)} %param.16) | copy-start | bytes 2322436
  25.7 0.6 copy-start.5
  28.8 23.0 %collective-permute-start.3 = (bf16[4,144,256]{2,1,0:T(8,128)(2,1)}, bf16[4,144,256]{2,1,0:T(8,128)(2,1)}, u32[]{:S(2)}, u32[]{:S(2)}) collective-permute-start(bf16[4,144,256]{2,1,0:T(8,128)(2,1)} %broadcast_select_fusion.6), channel_id=1, source_target_pairs={{0,1},{1,0},{2,3},{3,2},{4,5},{5,4},{6,7},{7,6},{8,9},{9,8},{10,11... | collective-permute-start | bytes 884744 | tf_op jit(solution)/shard_map/ppermute | solution.py:332
  31.8 20.0 %collective-permute-start.2 = (bf16[4,144,256]{2,1,0:T(8,128)(2,1)}, bf16[4,144,256]{2,1,0:T(8,128)(2,1)}, u32[]{:S(2)}, u32[]{:S(2)}) collective-permute-start(bf16[4,144,256]{2,1,0:T(8,128)(2,1)} %get-tuple-element.24), channel_id=1, source_target_pairs={{1,2},{2,1},{3,4},{4,3},{5,6},{6,5},{9,10},{10,9},{11,12},{12,11},... | collective-permute-start | bytes 884744 | tf_op jit(solution)/shard_map/ppermute | solution.py:333
  38.5 2.5 %copy-start = (bf16[9,256,256]{1,2,0:T(8,128)(2,1)S(1)}, bf16[9,256,256]{1,2,0:T(8,128)(2,1)}, u32[]{:S(2)}) copy-start(bf16[9,256,256]{1,2,0:T(8,128)(2,1)} %get-tuple-element.28) | copy-start | bytes 3538948
  42.5 1.6 %copy-start.6 = (bf16[22,168]{1,0:T(8,128)(2,1)S(1)}, bf16[22,168]{1,0:T(8,128)(2,1)}, u32[]{:S(2)}) copy-start(bf16[22,168]{1,0:T(8,128)(2,1)} %param.20) | copy-start | bytes 22180
  42.5 2.2 %copy-start.8 = (f32[22]{0:T(128)S(1)}, f32[22]{0:T(128)}, u32[]{:S(2)}) copy-start(f32[22]{0:T(128)} %param.21) | copy-start | bytes 268
  104.2 13.0 %collective-permute-start.4 = (bf16[576,256]{1,0:T(8,128)(2,1)S(1)}, bf16[576,256]{1,0:T(8,128)(2,1)S(1)}, u32[]{:S(2)}, u32[]{:S(2)}) collective-permute-start(bf16[576,256]{1,0:T(8,128)(2,1)S(1)} %get-tuple-element.40), channel_id=1, source_target_pairs={{1,2},{2,1},{3,4},{4,3},{5,6},{6,5},{9,10},{10,9},{11,12},{12,11},... | collective-permute-start | bytes 884744 | tf_op jit(solution)/shard_map/ppermute | solution.py:333
  107.1 16.3 %collective-permute-start.5 = (bf16[576,256]{1,0:T(8,128)(2,1)S(1)}, bf16[576,256]{1,0:T(8,128)(2,1)S(1)}, u32[]{:S(2)}, u32[]{:S(2)}) collective-permute-start(bf16[576,256]{1,0:T(8,128)(2,1)S(1)} %get-tuple-element.39), channel_id=1, source_target_pairs={{0,1},{1,0},{2,3},{3,2},{4,5},{5,4},{6,7},{7,6},{8,9},{9,8},{10,11... | collective-permute-start | bytes 884744 | tf_op jit(solution)/shard_map/ppermute | solution.py:332
  123.5 7.9 %copy-start.2 = (bf16[576,256]{1,0:T(8,128)(2,1)}, bf16[576,256]{1,0:T(8,128)(2,1)S(1)}, u32[]{:S(2)}) copy-start(bf16[576,256]{1,0:T(8,128)(2,1)S(1)} %get-tuple-element.37.below_ref) | copy-start | bytes 884740
  123.5 7.9 %copy-start.3 = (bf16[576,256]{1,0:T(8,128)(2,1)}, bf16[576,256]{1,0:T(8,128)(2,1)S(1)}, u32[]{:S(2)}) copy-start(bf16[576,256]{1,0:T(8,128)(2,1)S(1)} %get-tuple-element.38.above_ref) | copy-start | bytes 884740
  124.8 5.9 %collective-permute-start.6 = (bf16[16,8,256]{2,1,0:T(8,128)(2,1)S(1)}, bf16[16,8,256]{2,1,0:T(8,128)(2,1)S(1)}, u32[]{:S(2)}, u32[]{:S(2)}) collective-permute-start(bf16[16,8,256]{2,1,0:T(8,128)(2,1)S(1)} %broadcast_select_fusion.9), channel_id=1, source_target_pairs={{8,16},{16,8},{24,32},{32,24},{40,48},{48,40},{56,64},{64,56},{72,... | collective-permute-start | bytes 196616 | tf_op jit(solution)/shard_map/ppermute | solution.py:333
  128.0 2.6 %collective-permute-start.7 = (bf16[16,8,256]{2,1,0:T(8,128)(2,1)S(1)}, bf16[16,8,256]{2,1,0:T(8,128)(2,1)S(1)}, u32[]{:S(2)}, u32[]{:S(2)}) collective-permute-start(bf16[16,8,256]{2,1,0:T(8,128)(2,1)S(1)} %get-tuple-element.21), channel_id=1, source_target_pairs={{0,8},{8,0},{16,24},{24,16},{32,40},{40,32},{48,56},{56,48},{64,72... | collective-permute-start | bytes 196616 | tf_op jit(solution)/shard_map/ppermute | solution.py:332
where the time goes:
time: 138 us
  Pallas kernels  58.3 us (42%)
  starting transfers between devices  28.3 us (21%)
  local copies, waits for them, and re-layouts  19 us (14%)
  waiting for transfers between devices  19 us (14%)
  other arithmetic  11.5 us (8%)
  between operations  1.59 us (1%)
    pallas_call x1, Pallas kernels, backward_pass(): pl.pallas_call(backward_kernel, out_shape=(jax.ShapeDtypeStruct((rows, wi...  24.5 us
    pallas_call x1, Pallas kernels, forward_pass(): pl.pallas_call(forward_kernel, out_shape=(jax.ShapeDtypeStruct((rows, wid...  24.3 us
    ppermute x4, starting transfers between devices, exchange(): lax.ppermute(jnp.where(even, to_before, to_after), axis, swap_pairs(size,...  13.7 us
    ppermute x4, waiting for transfers between devices, exchange(): lax.ppermute(jnp.where(even, to_after, to_before), axis, swap_pairs(size,...  11.2 us
    all_to_all x1, starting transfers between devices, shards(): lax.all_to_all(packed.reshape(holders, CAPACITY * SLOT, cells), ('lon', '...  8.01 us
    ppermute x4, waiting for transfers between devices, exchange(): lax.ppermute(jnp.where(even, to_before, to_after), axis, swap_pairs(size,...  7.77 us
    transpose x4, local copies, waits for them, and re-layouts, shards(): turned = [jnp.transpose(kernel, (0, 2, 1)) for kernel in kernels]  7.24 us
    ppermute x4, starting transfers between devices, exchange(): lax.ppermute(jnp.where(even, to_after, to_before), axis, swap_pairs(size,...  6.54 us
  transfers between devices with their start and end apart: 9, of which 4 were waited for; matrix products, arithmetic and copies ran while one was open for 18% of the time, Pallas kernels for 20%

commit v1 on v0

v1 whole, which is shorter than its diff:
```python
import jax
import jax.numpy as jnp
from jax import lax
from jax.experimental import pallas as pl
from jax.experimental.pallas import tpu as pltpu
from jax.sharding import PartitionSpec as P


LAYERS = 4
CAPACITY = 2
HALO = 4
SIDE = 8
LANES = 256
SLOT = 24
BLOCK = 4
F32 = jnp.float32
BF16 = jnp.bfloat16


def vmem_specs(count):
    return [pl.BlockSpec(memory_space=pltpu.VMEM) for _ in range(count)]


def smem_spec():
    return pl.BlockSpec(memory_space=pltpu.SMEM)


def params(mebibytes):
    return pltpu.CompilerParams(vmem_limit_bytes=mebibytes << 20)


def near_core(*arrays):
    return [pltpu.with_memory_space_constraint(array, pltpu.VMEM) for array in arrays]


def in_hbm(*arrays):
    return [pltpu.with_memory_space_constraint(array, pltpu.HBM) for array in arrays]


def far_specs(count):
    return [pl.BlockSpec(memory_space=pl.ANY) for _ in range(count)]


def copies(pairs, sems):
    return [pltpu.make_async_copy(src, dst, sems.at[i]) for i, (src, dst) in enumerate(pairs)]


def pack_kernel(slot_ref, tile_ref, values_ref, out_ref, wide_ref):
    channels, count, width = values_ref.shape
    slots = out_ref.shape[0] // SLOT
    onehot = lax.broadcasted_iota(jnp.int32, (slots, count), 0) == slot_ref[...]
    onehot = onehot.astype(F32).astype(BF16)
    for k in range(channels):
        wide_ref[pl.ds(k, slots, stride=SLOT), :] = jnp.dot(
            onehot, values_ref[k], preferred_element_type=F32
        )
    numbers = jnp.broadcast_to((tile_ref[...] + 1).astype(F32), (count, width)).astype(BF16)
    placed = jnp.dot(onehot, numbers, preferred_element_type=F32)
    for k in range(channels, SLOT):
        wide_ref[pl.ds(k, slots, stride=SLOT), :] = placed
    out_ref[...] = wide_ref[...].astype(BF16)


def pack_blocks(slots, tiles, values, slot_count):
    width = values.shape[2]
    return pl.pallas_call(
        pack_kernel,
        out_shape=jax.ShapeDtypeStruct((slot_count * SLOT, width), BF16),
        in_specs=vmem_specs(3),
        out_specs=vmem_specs(1)[0],
        scratch_shapes=[pltpu.VMEM((slot_count * SLOT, width), F32)],
        compiler_params=params(12),
        name="pack_blocks",
    )(slots[None, :], tiles[:, None], jnp.transpose(values, (1, 0, 2)))


def put_shifted(dst_ref, row, width, act):
    size, channels = act.shape
    at = pl.ds(row * width, size)
    dst_ref[at, LANES : LANES + channels] = act.astype(BF16)
    dst_ref[at, 0:channels] = pltpu.roll(act, 1, 0).astype(BF16)
    dst_ref[at, 2 * LANES : 2 * LANES + channels] = pltpu.roll(act, size - 1, 0).astype(BF16)


def conv_block(src_ref, row, rows, width, w_ref, side, flip):
    acc = None
    taken = w_ref.shape[1 + side]
    for p in range(3):
        at = pl.ds((row + p) * width, rows * width)
        for q in range(3):
            tap = 3 * p + q
            part = lax.dot_general(
                src_ref[at, q * LANES : q * LANES + taken],
                w_ref[8 - tap if flip else tap],
                (((1,), (side,)), ((), ())),
                preferred_element_type=F32,
            )
            acc = part if acc is None else acc + part
    return acc


def conv_layer(rows, compute, finish, acc_a, acc_b):
    full, rest = divmod(rows, BLOCK)
    first = compute(0, BLOCK)
    size, channels = first.shape
    unit = size // BLOCK

    def keep(acc, value):
        acc[0 : value.shape[0], 0:channels] = value

    def kept(acc, n):
        return acc[0 : n * unit, 0:channels]

    keep(acc_a, first)
    pairs = (full - 1) // 2

    def body(j, carry):
        row = 2 * BLOCK * j
        keep(acc_b, compute(row + BLOCK, BLOCK))
        finish(row, BLOCK, kept(acc_a, BLOCK))
        keep(acc_a, compute(row + 2 * BLOCK, BLOCK))
        finish(row + BLOCK, BLOCK, kept(acc_b, BLOCK))
        return carry

    lax.fori_loop(0, pairs, body, 0)
    done = 2 * pairs
    last, free = acc_a, acc_b
    if full - 1 > done:
        keep(acc_b, compute((done + 1) * BLOCK, BLOCK))
        finish(done * BLOCK, BLOCK, kept(acc_a, BLOCK))
        last, free = acc_b, acc_a
    if rest:
        keep(free, compute(full * BLOCK, rest))
    finish((full - 1) * BLOCK, BLOCK, kept(last, BLOCK))
    if rest:
        finish(full * BLOCK, rest, kept(free, rest))


def either(flag, yes, no):
    return jnp.where(flag == 1, yes, no)


def turn_kernel(place_ref, state_ref, own_ref, near_ref, far_ref, low_ref, high_ref):
    _, rows, cells = state_ref.shape
    for r in range(rows):
        part = jnp.transpose(state_ref[:, r, :])
        own_ref[r * cells : (r + 1) * cells, :] = part.astype(BF16)
        low_ref[r * SIDE : (r + 1) * SIDE, :] = part[0:SIDE, :]
        high_ref[r * SIDE : (r + 1) * SIDE, :] = part[cells - SIDE : cells, :]
    low = low_ref[...]
    high = high_ref[...]
    near_ref[...] = either(place_ref[0], high, low).astype(BF16)
    far_ref[...] = either(place_ref[0], low, high).astype(BF16)


def turn_state(place, state):
    channels, rows, cells = state.shape
    edge = (rows * SIDE, channels)
    return pl.pallas_call(
        turn_kernel,
        out_shape=(
            pltpu.HBM((rows * cells, channels), BF16),
            jax.ShapeDtypeStruct(edge, BF16),
            jax.ShapeDtypeStruct(edge, BF16),
        ),
        in_specs=[smem_spec()] + vmem_specs(1),
        out_specs=tuple(vmem_specs(3)),
        scratch_shapes=[pltpu.VMEM(edge, F32)] * 2,
        compiler_params=params(8),
        name="turn_state",
    )(place, *near_core(state))


def framed_row(place_ref, own_ref, near_ref, far_ref, r, cells):
    at = pl.ds(r * SIDE, SIDE)
    near = near_ref[at, :].astype(F32)
    far = far_ref[at, :].astype(F32)
    own = own_ref[pl.ds(r * cells, cells), :].astype(F32)
    left = either(place_ref[0], far, near)
    right = either(place_ref[0], near, far)
    return jnp.concatenate([left, own, right], axis=0)


def frame_kernel(place_ref, own_ref, lon_near_ref, lon_far_ref, near_ref, far_ref):
    rows = lon_near_ref.shape[0] // SIDE
    cells = own_ref.shape[0] // rows
    width = cells + 2 * SIDE
    for i in range(HALO):
        top = framed_row(place_ref, own_ref, lon_near_ref, lon_far_ref, i, cells)
        low = framed_row(place_ref, own_ref, lon_near_ref, lon_far_ref, rows - HALO + i, cells)
        at = pl.ds(i * width, width)
        near_ref[at, :] = either(place_ref[1], low, top).astype(BF16)
        far_ref[at, :] = either(place_ref[1], top, low).astype(BF16)


def frame_rows(place, own, lon_near, lon_far, width):
    shape = (HALO * width, own.shape[1])
    return pl.pallas_call(
        frame_kernel,
        out_shape=(jax.ShapeDtypeStruct(shape, BF16),) * 2,
        in_specs=[smem_spec()] + vmem_specs(3),
        out_specs=tuple(vmem_specs(2)),
        compiler_params=params(8),
        name="frame_rows",
    )(place, *in_hbm(own), lon_near, lon_far)


def weight_scratch(weights):
    return [pltpu.VMEM(weight.shape, BF16) for weight in weights]


def forward_kernel(
    place_ref, own_ref, lon_near_ref, lon_far_ref, lat_near_ref, lat_far_ref, op_ref, w0_far, wm_far, w3_far,
    pre_far, pred_ref, d0_far, d1_far, d2_far,
    buf_a, buf_b, acc_a, acc_b, w0, wm, w3, pre_ref, d0, d1, d2, in_sems, out_sems,
):
    rows, width, _ = pre_ref.shape
    cells = width - 2 * SIDE
    weights = (w0, wm.at[0], wm.at[1], w3)
    slopes = (d0, d1, d2)
    loads = copies(
        ((w0_far, w0), (wm_far.at[0], wm.at[0]), (wm_far.at[1], wm.at[1]), (w3_far, w3)), in_sems
    )
    stores = copies(((d0, d0_far), (d1, d1_far), (d2, d2_far), (pre_ref, pre_far)), out_sems)
    for load in loads:
        load.start()

    def fill(i, carry):
        put_shifted(buf_a, i + HALO, width, framed_row(place_ref, own_ref, lon_near_ref, lon_far_ref, i, cells))
        return carry

    lax.fori_loop(0, rows, fill, 0)
    for i in range(HALO):
        at = pl.ds(i * width, width)
        near = lat_near_ref[at, :].astype(F32)
        far = lat_far_ref[at, :].astype(F32)
        put_shifted(buf_a, i, width, either(place_ref[1], far, near))
        put_shifted(buf_a, i + HALO + rows, width, either(place_ref[1], near, far))
    src, dst = buf_a, buf_b
    for layer in range(LAYERS):
        margin = HALO - 1 - layer
        count = rows + 2 * margin

        def compute(row, n, src=src, layer=layer):
            return conv_block(src, row, n, width, weights[layer], 0 if layer == 0 else 1, False)

        loads[layer].wait()

        if layer < LAYERS - 1:

            def finish(row, n, value, dst=dst, layer=layer):
                gate = 0.5 + 0.5 * jnp.tanh(0.5 * value)
                act = value * gate
                slope = gate + act * (1.0 - gate)
                slopes[layer][pl.ds(row * width, n * width), :] = slope.astype(BF16)
                put_shifted(dst, row, width, act)

        else:

            def finish(row, n, value):
                for i in range(n):
                    part = value[i * width : (i + 1) * width, :]
                    pre_ref[row + i] = part
                    own = own_ref[pl.ds((row + i) * cells, cells), :].astype(F32)
                    clean = (own + part[SIDE : SIDE + cells, :]).astype(BF16)
                    pred_ref[row + i] = lax.dot_general(
                        op_ref[...], clean, (((1,), (1,)), ((), ())), preferred_element_type=F32
                    )

        conv_layer(count, compute, finish, acc_a, acc_b)
        if layer < LAYERS - 1:
            size = margin * width

            def clear(first, dst=dst, layer=layer, size=size):
                slopes[layer][first : first + size, :] = jnp.zeros((size, LANES), BF16)
                dst[first : first + size, :] = jnp.zeros((size, 3 * LANES), BF16)

            @pl.when(place_ref[2] == 1)
            def _():
                clear(0)

            @pl.when(place_ref[3] == 1)
            def _(count=count, size=size):
                clear(count * width - size)

        stores[layer].start()
        src, dst = dst, src
    for store in stores:
        store.wait()


def forward_pass(place, own, lon, lat, weights, operator, rows, width):
    slopes = [((rows + 2 * (HALO - 1 - layer)) * width, LANES) for layer in range(LAYERS - 1)]
    pre = (rows, width, own.shape[1])
    padded = (rows + 2 * HALO) * width
    return pl.pallas_call(
        forward_kernel,
        out_shape=(
            pltpu.HBM(pre, F32),
            pltpu.HBM((rows, operator.shape[0], width - 2 * SIDE), F32),
        )
        + tuple(pltpu.HBM(shape, BF16) for shape in slopes),
        in_specs=[smem_spec()] + vmem_specs(6) + far_specs(3),
        out_specs=tuple(far_specs(1) + vmem_specs(1) + far_specs(3)),
        scratch_shapes=[pltpu.VMEM((padded, 3 * LANES), BF16)] * 2
        + [pltpu.VMEM((BLOCK * width, LANES), F32)] * 2
        + weight_scratch(weights)
        + [pltpu.VMEM(pre, F32)]
        + [pltpu.VMEM(shape, BF16) for shape in slopes]
        + [pltpu.SemaphoreType.DMA((LAYERS,)), pltpu.SemaphoreType.DMA((LAYERS,))],
        compiler_params=params(34),
        name="forward_pass",
    )(place, *in_hbm(own), *lon, *lat, operator, *in_hbm(*weights))


LEAD = HALO + 1


def slope_rows(layer, first):
    return first - (layer - HALO + 1)


def edge_kernel(
    place_ref, recv_ref, pred_ref, op_ref, prec_ref, d0_far, d1_far, d2_far, w0_far, wm_far, w3_far,
    pulled_ref, near_ref, far_ref, s0_ref, s1_ref, s2_ref,
    wide_ref, sums_ref, buf_a, buf_b, acc_a, acc_b, w0, wm, w3, d_ref, in_sems,
):
    rows, cells, channels = pulled_ref.shape
    width = cells + 2 * SIDE
    bands = 22
    slots = recv_ref.shape[0] // SLOT
    weights = (w0, wm.at[0], wm.at[1], w3)
    strips = (s0_ref, s1_ref, s2_ref)
    size = HALO * width
    pairs = [(w3_far, w3), (wm_far.at[1], wm.at[1]), (wm_far.at[0], wm.at[0]), (w0_far, w0)]
    for layer, source in ((2, d2_far), (1, d1_far), (0, d0_far)):
        for end in range(2):
            first = layer + 1 - HALO if end == 0 else rows - 1 - layer
            at = slope_rows(layer, first) * width
            pairs.append((source.at[pl.ds(at, size)], d_ref.at[layer, end]))
    loads = copies(pairs, in_sems)
    for load in loads:
        load.start()

    nothing = jnp.zeros((4 * width, 3 * LANES), BF16)
    buf_a[width : 5 * width, :] = nothing
    buf_a[(rows + 5) * width : (rows + 9) * width, :] = nothing
    buf_b[0 : 4 * width, :] = nothing
    buf_b[(rows + 6) * width : (rows + 10) * width, :] = nothing

    wide_ref[...] = recv_ref[...].astype(F32)
    sums_ref[...] = jnp.zeros(sums_ref.shape, F32)
    numbers = wide_ref[pl.ds(bands, slots, stride=SLOT), :]
    lane = lax.broadcasted_iota(jnp.int32, (slots, cells), 1).astype(F32) + 1.0
    onehot = jnp.transpose((numbers == lane).astype(F32))[0:rows, :].astype(BF16)
    held = jnp.dot(onehot, jnp.ones((slots, cells), BF16), preferred_element_type=F32)
    for k in range(bands):
        part = wide_ref[pl.ds(k, slots, stride=SLOT), :].astype(BF16)
        sums_ref[pl.ds(k, rows, stride=32), :] = jnp.dot(onehot, part, preferred_element_type=F32)
    for r in range(rows):
        summed = sums_ref[r * 32 : (r + 1) * 32, :]
        weighted = (summed - held[r : r + 1, :] * pred_ref[r]) * prec_ref[...]
        pulled = jnp.dot(
            jnp.transpose(weighted).astype(BF16), op_ref[...], preferred_element_type=F32
        )
        pulled_ref[r] = pulled
        if r < HALO or r >= rows - HALO:
            side = jnp.zeros((SIDE, channels), F32)
            put_shifted(buf_a, r + LEAD, width, jnp.concatenate([side, pulled, side], axis=0))

    src, dst = buf_a, buf_b
    for layer in range(LAYERS - 1, -1, -1):
        margin = LAYERS - layer
        tops = (-margin, rows + margin - HALO)
        accs = (acc_a, acc_b)
        loads[LAYERS - 1 - layer].wait()
        for end in range(2):
            value = conv_block(
                src, tops[end] + LEAD - 1, HALO, width, weights[layer], 1 if layer == 0 else 0, True
            )
            accs[end][:, 0 : value.shape[1]] = value
        if layer > 0:
            for end in range(2):
                loads[LAYERS + 2 * (LAYERS - 1 - layer) + end].wait()
                value = accs[end][...] * d_ref[layer - 1, end].astype(F32)
                put_shifted(dst, tops[end] + LEAD, width, value)
                half = size // 2
                kept = value[half:, :] if end == 0 else value[0:half, :]
                strips[layer - 1][end * half : (end + 1) * half, :] = kept.astype(BF16)
        else:
            top = acc_a[:, 0:channels]
            low = acc_b[:, 0:channels]
            near_ref[...] = either(place_ref[1], low, top).astype(BF16)
            far_ref[...] = either(place_ref[1], top, low).astype(BF16)
        src, dst = dst, src


def edge_pass(place, recv, pred, slopes, operator, precision, weights, channels):
    rows, cells = pred.shape[0], pred.shape[2]
    width = cells + 2 * SIDE
    padded = (rows + 2 * LEAD) * width
    size = HALO * width
    return pl.pallas_call(
        edge_kernel,
        out_shape=(
            pltpu.HBM((rows, cells, channels), F32),
            jax.ShapeDtypeStruct((size, channels), BF16),
            jax.ShapeDtypeStruct((size, channels), BF16),
        )
        + tuple(pltpu.HBM((size, LANES), BF16) for _ in range(LAYERS - 1)),
        in_specs=[smem_spec()] + vmem_specs(4) + far_specs(6),
        out_specs=tuple(vmem_specs(6)),
        scratch_shapes=[
            pltpu.VMEM(recv.shape, F32),
            pltpu.VMEM((rows * 32, recv.shape[1]), F32),
        ]
        + [pltpu.VMEM((padded, 3 * LANES), BF16)] * 2
        + [pltpu.VMEM((size, LANES), F32)] * 2
        + weight_scratch(weights)
        + [pltpu.VMEM((LAYERS - 1, 2, size, LANES), BF16), pltpu.SemaphoreType.DMA((LAYERS + 6,))],
        compiler_params=params(34),
        name="edge_pass",
    )(place, recv, *in_hbm(pred), operator, precision, *in_hbm(*slopes, *weights))


def inner_kernel(
    scale_ref, pulled_ref, s0_ref, s1_ref, s2_ref, pre_far, d0_far, d1_far, d2_far, w0_far, wm_far, w3_far,
    own_ref,
    buf_a, buf_b, acc_a, acc_b, w0, wm, w3, pre_ref, d0, d1, d2, in_sems,
):
    rows, cells, channels = pulled_ref.shape
    width = cells + 2 * SIDE
    weights = (w0, wm.at[0], wm.at[1], w3)
    strips = (s0_ref, s1_ref, s2_ref)
    slopes = (d0, d1, d2)
    pairs = [(w3_far, w3)]
    for layer, source, weight in ((2, d2_far, 1), (1, d1_far, 0), (0, d0_far, None)):
        first = layer + 1
        count = slopes[layer].shape[0]
        pairs.append((source.at[pl.ds(slope_rows(layer, first) * width, count)], slopes[layer]))
        pairs.append((w0_far, w0) if weight is None else (wm_far.at[weight], wm.at[weight]))
    pairs.append((pre_far, pre_ref))
    loads = copies(pairs, in_sems)
    for load in loads:
        load.start()

    def fill(r, carry):
        side = jnp.zeros((SIDE, channels), F32)
        put_shifted(buf_a, r + LEAD, width, jnp.concatenate([side, pulled_ref[r], side], axis=0))
        return carry

    lax.fori_loop(0, rows, fill, 0)
    loads[0].wait()
    src, dst = buf_a, buf_b
    half = HALO // 2 * width
    for layer in range(LAYERS - 1, -1, -1):
        begin = layer
        count = rows - 2 * layer

        def compute(row, n, src=src, layer=layer, begin=begin):
            return conv_block(
                src, row + begin + LEAD - 1, n, width, weights[layer], 1 if layer == 0 else 0, True
            )

        if layer > 0:
            kept = strips[layer - 1]
            put_shifted(dst, layer - 2 + LEAD, width, kept[0:half, :].astype(F32))
            put_shifted(dst, rows - layer + LEAD, width, kept[half:, :].astype(F32))
            loads[2 * (LAYERS - 1 - layer) + 1].wait()

            def finish(row, n, value, dst=dst, layer=layer, begin=begin):
                slope = slopes[layer - 1][pl.ds(row * width, n * width), :]
                put_shifted(dst, row + begin + LEAD, width, value * slope.astype(F32))

            conv_layer(count, compute, finish, acc_a, acc_b)
            loads[2 * (LAYERS - 1 - layer) + 2].wait()
        else:
            loads[-1].wait()

            def finish(row, n, value):
                side = jnp.zeros((SIDE, channels), F32)
                for i in range(n):
                    base = pre_ref[row + i][SIDE : SIDE + cells, :] * scale_ref[0] + pulled_ref[row + i]
                    base = jnp.concatenate([side, base, side], axis=0)
                    own_ref[row + i] = base + value[i * width : (i + 1) * width, :]

            conv_layer(count, compute, finish, acc_a, acc_b)
        src, dst = dst, src


def inner_pass(scale, pulled, strips, pre, slopes, weights):
    rows, width, channels = pre.shape
    padded = (rows + 2 * LEAD) * width
    kept = [((rows - 2 * (layer + 1)) * width, LANES) for layer in range(LAYERS - 1)]
    return pl.pallas_call(
        inner_kernel,
        out_shape=pltpu.HBM((rows, width, channels), F32),
        in_specs=[smem_spec()] + vmem_specs(4) + far_specs(7),
        out_specs=vmem_specs(1)[0],
        scratch_shapes=[pltpu.VMEM((padded, 3 * LANES), BF16)] * 2
        + [pltpu.VMEM((BLOCK * width, LANES), F32)] * 2
        + weight_scratch(weights)
        + [pltpu.VMEM(pre.shape, F32)]
        + [pltpu.VMEM(shape, BF16) for shape in kept]
        + [pltpu.SemaphoreType.DMA((2 * LAYERS,))],
        compiler_params=params(34),
        name="inner_pass",
    )(scale, *in_hbm(pulled, *strips, pre, *slopes, *weights))


def final_kernel(
    scale_ref, own_ref, above_ref, below_ref, left_ref, right_ref, state_ref, noise_ref, out_ref
):
    rows, width = own_ref.shape[0], own_ref.shape[1]
    cells = width - 2 * SIDE
    for r in range(rows):
        total = own_ref[r][SIDE : SIDE + cells, :]
        if r < HALO:
            total = total + above_ref[r * width : (r + 1) * width, :].astype(F32)[SIDE : SIDE + cells, :]
        if r >= rows - HALO:
            at = r - (rows - HALO)
            total = total + below_ref[at * width : (at + 1) * width, :].astype(F32)[SIDE : SIDE + cells, :]
        first = total[0:SIDE, :] + left_ref[r]
        last = total[cells - SIDE : cells, :] + right_ref[r]
        total = jnp.concatenate([first, total[SIDE : cells - SIDE, :], last], axis=0)
        turned = jnp.transpose(total)
        out_ref[:, r, :] = (
            state_ref[:, r, :] + scale_ref[0] * turned + scale_ref[1] * noise_ref[:, r, :]
        )


def final_pass(scale, own, above, below, left, right, state, noise):
    return pl.pallas_call(
        final_kernel,
        out_shape=jax.ShapeDtypeStruct(state.shape, F32),
        in_specs=[smem_spec()] + vmem_specs(7),
        out_specs=vmem_specs(1)[0],
        compiler_params=params(16),
        name="final_pass",
    )(scale, *in_hbm(own), above, below, left, right, *near_core(state, noise))


def swap_pairs(size, first, wrap):
    pairs = []
    for low in range(first, size if wrap else size - 1, 2):
        high = (low + 1) % size
        pairs += [(low, high), (high, low)]
    return pairs


def swap(axis, wrap, near, far):
    size = lax.axis_size(axis)
    return lax.ppermute(near, axis, swap_pairs(size, 0, wrap)), lax.ppermute(far, axis, swap_pairs(size, 1, wrap))


def exchange(axis, wrap, to_before, to_after):
    even = lax.axis_index(axis) % 2 == 0
    near, far = swap(axis, wrap, jnp.where(even, to_after, to_before), jnp.where(even, to_before, to_after))
    return jnp.where(even, far, near), jnp.where(even, near, far)


def pad_to(values, shape):
    return jnp.pad(values, [(0, n - m) for m, n in zip(values.shape, shape)])


def shards(
    state,
    noise,
    first_kernel,
    middle_kernels,
    last_kernel,
    obs_values,
    obs_holder,
    obs_tile,
    obs_operator,
    obs_precision,
    noise_level,
    step_size,
):
    channels, rows, cells = state.shape
    width = cells + 2 * SIDE
    weights = (jnp.transpose(first_kernel, (0, 2, 1)), middle_kernels, last_kernel)
    lon, lat = lax.axis_index("lon"), lax.axis_index("lat")
    bands = lax.axis_size("lat")
    place = jnp.stack([lon % 2 == 0, lat % 2 == 0, lat == 0, lat == bands - 1]).astype(jnp.int32)

    targets = obs_holder[:, 0]
    count = targets.shape[0]
    positions = lax.broadcasted_iota(jnp.int32, (count, count), 0)
    earlier = lax.broadcasted_iota(jnp.int32, (count, count), 1)
    before = (targets[:, None] == targets[None, :]) & (earlier < positions)
    slots = targets * CAPACITY + jnp.sum(before.astype(jnp.int32), axis=1)
    holders = lax.axis_size(("lon", "lat"))
    packed = pack_blocks(slots, obs_tile, obs_values, holders * CAPACITY)
    own, *edges = turn_state(place, state)
    lon_halo = swap("lon", True, *edges)
    framed = frame_rows(place, own, *lon_halo, width)
    packed, framed = lax.optimization_barrier((packed, framed))
    lat_halo = swap("lat", False, *framed)
    recv = lax.all_to_all(
        packed.reshape(holders, CAPACITY * SLOT, cells), ("lon", "lat"), split_axis=0, concat_axis=0, tiled=True
    ).reshape(packed.shape)

    operator = pad_to(obs_operator, (32, channels))
    precision = pad_to(obs_precision[:, None], (32, 1))
    pre, pred, *slopes = forward_pass(place, own, lon_halo, lat_halo, weights, operator, rows, width)
    inverse = (1.0 / (noise_level * noise_level)).astype(F32)
    pulled, near, far, *strips = edge_pass(
        place, recv, pred, slopes, operator, precision, weights, channels
    )
    near, far = swap("lat", False, near, far)
    own = inner_pass(inverse, pulled, strips, pre, slopes, weights)
    even = place[1] == 1
    above, below = jnp.where(even, far, near), jnp.where(even, near, far)
    above_side = above.reshape(HALO, width, channels)
    below_side = below.reshape(HALO, width, channels)

    def edge(at):
        added = [
            above_side[:, at : at + SIDE].astype(F32),
            jnp.zeros((rows - 2 * HALO, SIDE, channels), F32),
            below_side[:, at : at + SIDE].astype(F32),
        ]
        return (own[:, at : at + SIDE] + jnp.concatenate(added, axis=0)).astype(BF16)

    left, right = exchange("lon", True, edge(0), edge(width - SIDE))
    scale = jnp.stack([step_size[0], jnp.sqrt(2.0 * step_size[0])])
    return final_pass(scale, own, above, below, left.astype(F32), right.astype(F32), state, noise)


def solution(mesh):
    placed = (
        P(None, "lat", "lon"),
        P(None, "lat", "lon"),
        P(),
        P(),
        P(),
        P(("lon", "lat"), None, None),
        P(("lon", "lat"), None),
        P(("lon", "lat")),
        P(),
        P(),
        P(),
        P(),
    )

    return jax.shard_map(
        shards, mesh=mesh, in_specs=placed, out_specs=P(None, "lat", "lon"), check_vma=False
    )
```

time: 138 us -> 127 us (0.920)
  the two profiles are of different devices: /device:TPU:2 before, /device:TPU:6 now
where the time goes in v1:
time: 127 us; the launch traced here: 126 us
  Pallas kernels  61.5 us (48%)
  waiting for transfers between devices  28.9 us (23%)
  starting transfers between devices  27.5 us (22%)
  other arithmetic  2.97 us (2%)
  local copies, waits for them, and re-layouts  2.95 us (2%)
  between operations  2.22 us (2%)
    ppermute x4, waiting for transfers between devices, swap(): lax.ppermute(near, axis, swap_pairs(size, 0, wrap))  26.8 us
    pallas_call x1, Pallas kernels, forward_pass(): pl.pallas_call(forward_kernel, out_shape=(pltpu.HBM(pre, F32), pltpu.HBM(...  23.4 us
    ppermute x4, starting transfers between devices, swap(): lax.ppermute(far, axis, swap_pairs(size, 1, wrap))  17.6 us
    pallas_call x1, Pallas kernels, inner_pass(): pl.pallas_call(inner_kernel, out_shape=pltpu.HBM((rows, width, channels),...  16.5 us
    pallas_call x1, Pallas kernels, edge_pass(): pl.pallas_call(edge_kernel, out_shape=(pltpu.HBM((rows, cells, channels),...  10.5 us
    all_to_all x1, starting transfers between devices, shards(): lax.all_to_all(packed.reshape(holders, CAPACITY * SLOT, cells), ('lon', '...  6.71 us
    pallas_call x1, Pallas kernels, final_pass(): pl.pallas_call(final_kernel, out_shape=jax.ShapeDtypeStruct(state.shape,...  5.3 us
    ppermute x4, starting transfers between devices, swap(): lax.ppermute(near, axis, swap_pairs(size, 0, wrap))  3.25 us
  transfers between devices with their start and end apart: 9, of which 2 were waited for; matrix products, arithmetic and copies ran while one was open for 3% of the time, Pallas kernels for 33%

profile of v1, /device:TPU:6, one launch (start us, length us, event | category | flops | bytes accessed | tf_op | source)
XLA Modules:
  0.0 126.1 jit_solution(12848509912969146269)
XLA Ops:
  0.0 0.1 add_convert_fusion.place_ref
  0.1 1.3 %copy-done = f32[168,16,128]{2,1,0:T(8,128)S(1)} copy-done((f32[168,16,128]{2,1,0:T(8,128)S(1)}, f32[168,16,128]{2,1,0:T(8,128)}, u32[]{:S(2)}) %copy-start) | copy-done | bytes 1376280
  1.4 2.3 %turn_state.1 = (bf16[2048,168]{1,0:T(8,128)(2,1)}, bf16[128,168]{1,0:T(8,128)(2,1)S(1)}, bf16[128,168]{1,0:T(8,128)(2,1)S(1)}) custom-call(s32[4]{0:T(128)S(1)} %add_convert_fusion.place_ref, f32[168,16,128]{2,1,0:T(8,128)S(1)} %copy-done), custom_call_target="tpu_custom_call" | custom-call | tf_op jit(solution)/shard_map/turn_state/pallas_call | solution.py:159
  3.8 0.0 collective-permute-start
  3.8 5.2 %collective-permute-start.1 = (bf16[128,168]{1,0:T(8,128)(2,1)S(1)}, bf16[128,168]{1,0:T(8,128)(2,1)S(1)}, u32[]{:S(2)}, u32[]{:S(2)}) collective-permute-start(bf16[128,168]{1,0:T(8,128)(2,1)S(1)} %get-tuple-element.26), channel_id=1, source_target_pairs={{8,16},{16,8},{24,32},{32,24},{40,48},{48,40},{56,64},{64,56},{72,... | collective-permute-start | bytes 129032 | tf_op jit(solution)/shard_map/ppermute | solution.py:553
  8.9 0.9 convert_reduce_fusion
  9.8 0.7 bitcast_add_fusion.slot_ref
  10.5 0.8 copy.15.tile_ref
  11.3 2.1 %pack_blocks.1 = bf16[6144,128]{1,0:T(8,128)(2,1)} custom-call(s32[1,96]{1,0:T(1,128)S(1)} %bitcast_add_fusion.slot_ref, s32[96,1]{1,0:T(8,128)S(1)} %copy.15.tile_ref, bf16[22,96,128]{2,1,0:T(8,128)(2,1)S(1)} %bitcast.21), custom_call_target="tpu_custom_call" | custom-call | tf_op jit(solution)/shard_map/pack_blocks/pallas_call | solution.py:66
  13.4 0.0 collective-permute-done.lon_near_ref
  13.4 1.4 %frame_rows.1 = (bf16[576,168]{1,0:T(8,128)(2,1)S(1)}, bf16[576,168]{1,0:T(8,128)(2,1)S(1)}) custom-call(s32[4]{0:T(128)S(1)} %add_convert_fusion.place_ref, bf16[2048,168]{1,0:T(8,128)(2,1)} %get-tuple-element.24.own_ref, bf16[128,168]{1,0:T(8,128)(2,1)S(1)} %collective-permute-done.lon_near_ref, bf16[128,168]{1,0:T(8,128)(2,1)S(1)} %collective-permute-done.1.lon_far_ref), custom_call_target="tpu_custom_call" | custom-call | tf_op jit(solution)/shard_map/frame_rows/pallas_call | solution.py:198
  14.7 0.0 copy-start.5
  14.7 0.0 copy-start.4
  14.8 6.7 %all-to-all-start = ((bf16[128,48,128]{2,1,0:T(8,128)(2,1)}), bf16[128,48,128]{2,1,0:T(8,128)(2,1)S(1)}, u32[]{:S(2)}, u32[]{:S(2)}) async-start(bf16[128,48,128]{2,1,0:T(8,128)(2,1)} %bitcast.9), calls=%async_computation | async-start | bytes 3145728 | tf_op jit(solution)/shard_map/all_to_all | solution.py:600
  21.5 3.1 %collective-permute-start.2 = (bf16[576,168]{1,0:T(8,128)(2,1)S(1)}, bf16[576,168]{1,0:T(8,128)(2,1)S(1)}, u32[]{:S(2)}, u32[]{:S(2)}) collective-permute-start(bf16[576,168]{1,0:T(8,128)(2,1)S(1)} %get-tuple-element.30), channel_id=1, source_target_pairs={{0,1},{1,0},{2,3},{3,2},{4,5},{5,4},{6,7},{7,6},{8,9},{9,8},{10,11... | collective-permute-start | bytes 580616 | tf_op jit(solution)/shard_map/ppermute | solution.py:553
  24.6 2.7 %collective-permute-start.3 = (bf16[576,168]{1,0:T(8,128)(2,1)S(1)}, bf16[576,168]{1,0:T(8,128)(2,1)S(1)}, u32[]{:S(2)}, u32[]{:S(2)}) collective-permute-start(bf16[576,168]{1,0:T(8,128)(2,1)S(1)} %get-tuple-element.31), channel_id=1, source_target_pairs={{1,2},{2,1},{3,4},{4,3},{5,6},{6,5},{9,10},{10,9},{11,12},{12,11},... | collective-permute-start | bytes 580616 | tf_op jit(solution)/shard_map/ppermute | solution.py:553
  27.3 0.1 copy.16
  27.4 26.8 %collective-permute-done.2.lat_near_ref = bf16[576,168]{1,0:T(8,128)(2,1)S(1)} collective-permute-done((bf16[576,168]{1,0:T(8,128)(2,1)S(1)}, bf16[576,168]{1,0:T(8,128)(2,1)S(1)}, u32[]{:S(2)}, u32[]{:S(2)}) %collective-permute-start.2) | collective-permute-done | bytes 193568 | tf_op jit(solution)/shard_map/ppermute | solution.py:553
  54.2 23.4 %forward_pass.1 = (f32[16,144,168]{2,1,0:T(8,128)}, f32[16,32,128]{2,1,0:T(8,128)}, bf16[3168,256]{1,0:T(8,128)(2,1)}, bf16[2880,256]{1,0:T(8,128)(2,1)}, bf16[2592,256]{1,0:T(8,128)(2,1)}) custom-call(s32[4]{0:T(128)S(1)} %add_convert_fusion.place_ref, bf16[2048,168]{1,0:T(8,128)(2,1)} %get-tuple-element.24.own_ref, ...), custom_call_target="tpu_custom_call" | custom-call | tf_op jit(solution)/shard_map/forward_pass/pallas_call | solution.py:296
  77.7 10.5 %edge_pass.1 = (f32[16,128,168]{2,1,0:T(8,128)}, bf16[576,168]{1,0:T(8,128)(2,1)S(1)}, bf16[576,168]{1,0:T(8,128)(2,1)S(1)}, bf16[576,256]{1,0:T(8,128)(2,1)}, b...) custom-call(s32[4]{0:T(128)S(1)} %add_convert_fusion.place_ref, bf16[6144,128]{1,0:T(8,128)(2,1)S(1)} %bitcast.18, ...), custom_call_target="tpu_custom_call" | custom-call | tf_op jit(solution)/shard_map/edge_pass/pallas_call | solution.py:403
  88.2 0.1 collective-permute-start.5
  88.2 5.9 %collective-permute-start.4 = (bf16[576,168]{1,0:T(8,128)(2,1)S(1)}, bf16[576,168]{1,0:T(8,128)(2,1)S(1)}, u32[]{:S(2)}, u32[]{:S(2)}) collective-permute-start(bf16[576,168]{1,0:T(8,128)(2,1)S(1)} %get-tuple-element.41), channel_id=1, source_target_pairs={{1,2},{2,1},{3,4},{4,3},{5,6},{6,5},{9,10},{10,9},{11,12},{12,11},... | collective-permute-start | bytes 580616 | tf_op jit(solution)/shard_map/ppermute | solution.py:553
  94.2 0.6 slice.21
  96.9 0.1 pad.14.clone
  96.9 16.5 %inner_pass.1.own_ref = f32[16,144,168]{2,1,0:T(8,128)} custom-call(f32[1]{0:T(128)S(6)} %div.3.scale_ref, f32[16,128,168]{2,1,0:T(8,128)} %get-tuple-element.36.pulled_ref, bf16[576,256]{1,0:T(8,128)(2,1)} %get-tuple-element.37.s0_ref, bf16[576,256]{1,0:T(8,128)(2,1)} %get-tuple-element.38.s1_ref, bf16[576,256]{1,0:T(8,128)(2,1)} %get-tuple-element.39.s2_ref, ...), custom_call_target="tpu_custom_call" | custom-call | tf_op jit(solution)/shard_map/inner_pass/pallas_call | solution.py:495
  113.5 0.0 copy-start.1
  113.6 1.2 broadcast_select_fusion.2
  114.7 0.1 collective-permute-start.7
  114.8 3.7 %collective-permute-start.6 = (bf16[16,8,168]{2,1,0:T(8,128)(2,1)S(1)}, bf16[16,8,168]{2,1,0:T(8,128)(2,1)S(1)}, u32[]{:S(2)}, u32[]{:S(2)}) collective-permute-start(bf16[16,8,168]{2,1,0:T(8,128)(2,1)S(1)} %broadcast_select_fusion.3), channel_id=1, source_target_pairs={{8,16},{16,8},{24,32},{32,24},{40,48},{48,40},{56,64},{64,56},{72,... | collective-permute-start | bytes 129032 | tf_op jit(solution)/shard_map/ppermute | solution.py:553
  118.6 0.1 pad_maximum_fusion.scale_ref
  118.6 2.1 %collective-permute-done.6 = bf16[16,8,168]{2,1,0:T(8,128)(2,1)S(1)} collective-permute-done((bf16[16,8,168]{2,1,0:T(8,128)(2,1)S(1)}, bf16[16,8,168]{2,1,0:T(8,128)(2,1)S(1)}, u32[]{:S(2)}, u32[]{:S(2)}) %collective-permute-start.6) | collective-permute-done | bytes 43040 | tf_op jit(solution)/shard_map/ppermute | solution.py:553
  120.8 5.3 %final_pass.1 = f32[168,16,128]{2,1,0:T(8,128)} custom-call(f32[2]{0:T(128)S(1)} %pad_maximum_fusion.scale_ref, f32[16,144,168]{2,1,0:T(8,128)} %inner_pass.1.own_ref, bf16[576,168]{1,0:T(8,128)(2,1)S(1)} %get-tuple-element.47.above_ref, bf16[576,168]{1,0:T(8,128)(2,1)S(1)} %get-tuple-element.46.below_ref, f32[16,8,168]{2,1,0:T(8,128)S(1)} %get-tuple-element.53.left_ref, ...), custom_call_target="tpu_custom_call" | custom-call | tf_op jit(solution)/shard_map/final_pass/pallas_call | solution.py:533
  (21 shorter events, 0.1 us)
Async XLA Ops:
  0.1 1.3 %copy-start = (f32[168,16,128]{2,1,0:T(8,128)S(1)}, f32[168,16,128]{2,1,0:T(8,128)}, u32[]{:S(2)}) copy-start(f32[168,16,128]{2,1,0:T(8,128)} %state_ref.3) | copy-start | bytes 4128772
  1.4 9.8 %copy-start.3 = (bf16[96,22,128]{2,0,1:T(8,128)(2,1)S(1)}, bf16[96,22,128]{2,0,1:T(8,128)(2,1)}, u32[]{:S(2)}) copy-start(bf16[96,22,128]{2,0,1:T(8,128)(2,1)} %param.17) | copy-start | bytes 1622020
  3.8 9.6 %collective-permute-start = (bf16[128,168]{1,0:T(8,128)(2,1)S(1)}, bf16[128,168]{1,0:T(8,128)(2,1)S(1)}, u32[]{:S(2)}, u32[]{:S(2)}) collective-permute-start(bf16[128,168]{1,0:T(8,128)(2,1)S(1)} %get-tuple-element.25), channel_id=1, source_target_pairs={{0,8},{8,0},{16,24},{24,16},{32,40},{40,32},{48,56},{56,48},{64,72... | collective-permute-start | bytes 129032 | tf_op jit(solution)/shard_map/ppermute | solution.py:553
  3.8 9.6 %collective-permute-start.1 = (bf16[128,168]{1,0:T(8,128)(2,1)S(1)}, bf16[128,168]{1,0:T(8,128)(2,1)S(1)}, u32[]{:S(2)}, u32[]{:S(2)}) collective-permute-start(bf16[128,168]{1,0:T(8,128)(2,1)S(1)} %get-tuple-element.26), channel_id=1, source_target_pairs={{8,16},{16,8},{24,32},{32,24},{40,48},{48,40},{56,64},{64,56},{72,... | collective-permute-start | bytes 129032 | tf_op jit(solution)/shard_map/ppermute | solution.py:553
  14.7 12.6 %copy-start.5 = (f32[22]{0:T(128)S(1)}, f32[22]{0:T(128)}, u32[]{:S(2)}) copy-start(f32[22]{0:T(128)} %param.21) | copy-start | bytes 268
  14.7 12.7 %copy-start.4 = (bf16[22,168]{1,0:T(8,128)(2,1)S(1)}, bf16[22,168]{1,0:T(8,128)(2,1)}, u32[]{:S(2)}) copy-start(bf16[22,168]{1,0:T(8,128)(2,1)} %param.20) | copy-start | bytes 22180
  14.8 62.9 %all-to-all-start = ((bf16[128,48,128]{2,1,0:T(8,128)(2,1)}), bf16[128,48,128]{2,1,0:T(8,128)(2,1)S(1)}, u32[]{:S(2)}, u32[]{:S(2)}) async-start(bf16[128,48,128]{2,1,0:T(8,128)(2,1)} %bitcast.9), calls=%async_computation | async-start | bytes 3145728 | tf_op jit(solution)/shard_map/all_to_all | solution.py:600
  21.5 32.8 %collective-permute-start.2 = (bf16[576,168]{1,0:T(8,128)(2,1)S(1)}, bf16[576,168]{1,0:T(8,128)(2,1)S(1)}, u32[]{:S(2)}, u32[]{:S(2)}) collective-permute-start(bf16[576,168]{1,0:T(8,128)(2,1)S(1)} %get-tuple-element.30), channel_id=1, source_target_pairs={{0,1},{1,0},{2,3},{3,2},{4,5},{5,4},{6,7},{7,6},{8,9},{9,8},{10,11... | collective-permute-start | bytes 580616 | tf_op jit(solution)/shard_map/ppermute | solution.py:553
  24.6 29.7 %collective-permute-start.3 = (bf16[576,168]{1,0:T(8,128)(2,1)S(1)}, bf16[576,168]{1,0:T(8,128)(2,1)S(1)}, u32[]{:S(2)}, u32[]{:S(2)}) collective-permute-start(bf16[576,168]{1,0:T(8,128)(2,1)S(1)} %get-tuple-element.31), channel_id=1, source_target_pairs={{1,2},{2,1},{3,4},{4,3},{5,6},{6,5},{9,10},{10,9},{11,12},{12,11},... | collective-permute-start | bytes 580616 | tf_op jit(solution)/shard_map/ppermute | solution.py:553
  88.2 25.3 %collective-permute-start.5 = (bf16[576,168]{1,0:T(8,128)(2,1)S(1)}, bf16[576,168]{1,0:T(8,128)(2,1)S(1)}, u32[]{:S(2)}, u32[]{:S(2)}) collective-permute-start(bf16[576,168]{1,0:T(8,128)(2,1)S(1)} %get-tuple-element.42), channel_id=1, source_target_pairs={{0,1},{1,0},{2,3},{3,2},{4,5},{5,4},{6,7},{7,6},{8,9},{9,8},{10,11... | collective-permute-start | bytes 580616 | tf_op jit(solution)/shard_map/ppermute | solution.py:553
  88.2 25.2 %collective-permute-start.4 = (bf16[576,168]{1,0:T(8,128)(2,1)S(1)}, bf16[576,168]{1,0:T(8,128)(2,1)S(1)}, u32[]{:S(2)}, u32[]{:S(2)}) collective-permute-start(bf16[576,168]{1,0:T(8,128)(2,1)S(1)} %get-tuple-element.41), channel_id=1, source_target_pairs={{1,2},{2,1},{3,4},{4,3},{5,6},{6,5},{9,10},{10,9},{11,12},{12,11},... | collective-permute-start | bytes 580616 | tf_op jit(solution)/shard_map/ppermute | solution.py:553
  96.9 23.8 %copy-start.2 = (f32[168,16,128]{2,1,0:T(8,128)S(1)}, f32[168,16,128]{2,1,0:T(8,128)}, u32[]{:S(2)}) copy-start(f32[168,16,128]{2,1,0:T(8,128)} %noise_ref.1) | copy-start | bytes 4128772
  113.5 7.3 %copy-start.1 = (f32[168,16,128]{2,1,0:T(8,128)S(1)}, f32[168,16,128]{2,1,0:T(8,128)}, u32[]{:S(2)}) copy-start(f32[168,16,128]{2,1,0:T(8,128)} %state_ref.3) | copy-start | bytes 4128772
  114.7 3.9 %collective-permute-start.7 = (bf16[16,8,168]{2,1,0:T(8,128)(2,1)S(1)}, bf16[16,8,168]{2,1,0:T(8,128)(2,1)S(1)}, u32[]{:S(2)}, u32[]{:S(2)}) collective-permute-start(bf16[16,8,168]{2,1,0:T(8,128)(2,1)S(1)} %get-tuple-element.43), channel_id=1, source_target_pairs={{0,8},{8,0},{16,24},{24,16},{32,40},{40,32},{48,56},{56,48},{64,72... | collective-permute-start | bytes 129032 | tf_op jit(solution)/shard_map/ppermute | solution.py:553
  114.8 5.9 %collective-permute-start.6 = (bf16[16,8,168]{2,1,0:T(8,128)(2,1)S(1)}, bf16[16,8,168]{2,1,0:T(8,128)(2,1)S(1)}, u32[]{:S(2)}, u32[]{:S(2)}) collective-permute-start(bf16[16,8,168]{2,1,0:T(8,128)(2,1)S(1)} %broadcast_select_fusion.3), channel_id=1, source_target_pairs={{8,16},{16,8},{24,32},{32,24},{40,48},{48,40},{56,64},{64,56},{72,... | collective-permute-start | bytes 129032 | tf_op jit(solution)/shard_map/ppermute | solution.py:553

commit v2 on v1

--- a/solution.py
+++ b/solution.py
@@ -1,3 +1,5 @@
+import functools
+
 import jax
 import jax.numpy as jnp
 from jax import lax
@@ -45,33 +47,61 @@
     return [pltpu.make_async_copy(src, dst, sems.at[i]) for i, (src, dst) in enumerate(pairs)]
 
 
-def pack_kernel(slot_ref, tile_ref, values_ref, out_ref, wide_ref):
-    channels, count, width = values_ref.shape
+BANDS = 22
+EDGE = 4
+
+
+def pack_kernel(holder_ref, tile_ref, values_ref, out_ref, wide_ref, *, shift):
+    count, width = values_ref.shape[1], values_ref.shape[2]
     slots = out_ref.shape[0] // SLOT
-    onehot = lax.broadcasted_iota(jnp.int32, (slots, count), 0) == slot_ref[...]
+    named = jnp.broadcast_to(holder_ref[...].astype(F32), (count, count))
+    first = lax.broadcasted_iota(jnp.int32, (count, count), 0)
+    second = lax.broadcasted_iota(jnp.int32, (count, count), 1)
+    same = (jnp.transpose(named) == named) & (first < second)
+    ranks = jnp.sum(same.astype(F32), axis=0, keepdims=True)
+    chosen = holder_ref[...] * CAPACITY + ranks.astype(jnp.int32)
+    onehot = lax.broadcasted_iota(jnp.int32, (slots, count), 0) == chosen
     onehot = onehot.astype(F32).astype(BF16)
-    for k in range(channels):
-        wide_ref[pl.ds(k, slots, stride=SLOT), :] = jnp.dot(
-            onehot, values_ref[k], preferred_element_type=F32
-        )
-    numbers = jnp.broadcast_to((tile_ref[...] + 1).astype(F32), (count, width)).astype(BF16)
-    placed = jnp.dot(onehot, numbers, preferred_element_type=F32)
-    for k in range(channels, SLOT):
-        wide_ref[pl.ds(k, slots, stride=SLOT), :] = placed
+    numbers = jnp.broadcast_to((tile_ref[...] + 1).astype(F32), (width, count))
+    numbers = jnp.transpose(numbers).astype(BF16)
+    cell = lax.broadcasted_iota(jnp.int32, (width, 2 * width), 0)
+    lane = lax.broadcasted_iota(jnp.int32, (width, 2 * width), 1)
+    high = lane - (cell - (width - EDGE)) * SLOT
+    low = lane - width - cell * SLOT
+    channel = jnp.where(
+        lane < width, jnp.where(cell >= width - EDGE, high, -1), jnp.where(cell < EDGE, low, -1)
+    )
+    edges = None
+    for k in range(BANDS + 1):
+        values = values_ref[k] if k < BANDS else numbers
+        if k < BANDS:
+            wide_ref[pl.ds(k, slots, stride=SLOT), :] = jnp.dot(
+                onehot, values, preferred_element_type=F32
+            )
+        spread = (channel == k).astype(F32).astype(BF16)
+        part = jnp.dot(values, spread, preferred_element_type=F32)
+        edges = part if edges is None else edges + part
+    placed = jnp.dot(onehot, edges.astype(BF16), preferred_element_type=F32)
+    own = jnp.dot(onehot, numbers, preferred_element_type=F32)
+    before = pltpu.roll(placed[:, 0:width], shift, 0)
+    after = pltpu.roll(placed[:, width : 2 * width], slots - shift, 0)
+    at = lax.broadcasted_iota(jnp.int32, (slots, width), 1)
+    wide_ref[pl.ds(BANDS, slots, stride=SLOT), :] = jnp.where(at == BANDS + 1, own, before)
+    wide_ref[pl.ds(BANDS + 1, slots, stride=SLOT), :] = after
     out_ref[...] = wide_ref[...].astype(BF16)
 
 
-def pack_blocks(slots, tiles, values, slot_count):
+def pack_blocks(holders, tiles, values, slot_count, shift):
     width = values.shape[2]
     return pl.pallas_call(
-        pack_kernel,
+        functools.partial(pack_kernel, shift=shift),
         out_shape=jax.ShapeDtypeStruct((slot_count * SLOT, width), BF16),
         in_specs=vmem_specs(3),
         out_specs=vmem_specs(1)[0],
         scratch_shapes=[pltpu.VMEM((slot_count * SLOT, width), F32)],
         compiler_params=params(12),
         name="pack_blocks",
-    )(slots[None, :], tiles[:, None], jnp.transpose(values, (1, 0, 2)))
+    )(holders.reshape(1, -1), tiles.reshape(1, -1), jnp.transpose(values, (1, 0, 2)))
 
 
 def put_shifted(dst_ref, row, width, act):
@@ -211,10 +241,10 @@
 
 def forward_kernel(
     place_ref, own_ref, lon_near_ref, lon_far_ref, lat_near_ref, lat_far_ref, op_ref, w0_far, wm_far, w3_far,
-    pre_far, pred_ref, d0_far, d1_far, d2_far,
-    buf_a, buf_b, acc_a, acc_b, w0, wm, w3, pre_ref, d0, d1, d2, in_sems, out_sems,
+    pre_far, pred_ref, edge_ref, d0_far, d1_far, d2_far,
+    buf_a, buf_b, acc_a, acc_b, w0, wm, w3, pre_ref, clean_a, clean_b, d0, d1, d2, in_sems, out_sems,
 ):
-    rows, width, _ = pre_ref.shape
+    rows, width, channels = pre_ref.shape
     cells = width - 2 * SIDE
     weights = (w0, wm.at[0], wm.at[1], w3)
     slopes = (d0, d1, d2)
@@ -261,10 +291,16 @@
                 for i in range(n):
                     part = value[i * width : (i + 1) * width, :]
                     pre_ref[row + i] = part
-                    own = own_ref[pl.ds((row + i) * cells, cells), :].astype(F32)
-                    clean = (own + part[SIDE : SIDE + cells, :]).astype(BF16)
+                    own = framed_row(place_ref, own_ref, lon_near_ref, lon_far_ref, row + i, cells)
+                    clean = (own + part).astype(BF16)
+                    at = pl.ds((row + i) * width, width)
+                    clean_a[at, :] = clean[:, 0:128].astype(F32)
+                    clean_b[at, 0 : channels - 128] = clean[:, 128:channels].astype(F32)
                     pred_ref[row + i] = lax.dot_general(
-                        op_ref[...], clean, (((1,), (1,)), ((), ())), preferred_element_type=F32
+                        op_ref[:, 0:channels],
+                        clean[SIDE : SIDE + cells, :],
+                        (((1,), (1,)), ((), ())),
+                        preferred_element_type=F32,
                     )
 
         conv_layer(count, compute, finish, acc_a, acc_b)
@@ -285,6 +321,18 @@
 
         stores[layer].start()
         src, dst = dst, src
+    tall = jnp.concatenate([op_ref[:, 0:channels].astype(F32), jnp.zeros((96, channels), F32)], axis=0).astype(BF16)
+    for end, first in ((0, SIDE - EDGE), (1, SIDE + cells)):
+        total = None
+        for c in range(EDGE):
+            at = pl.ds(first + c, rows, stride=width)
+            clean = jnp.concatenate([clean_a[at, :], clean_b[at, :]], axis=1)[:, 0:channels]
+            part = lax.dot_general(
+                clean.astype(BF16), tall, (((1,), (1,)), ((), ())), preferred_element_type=F32
+            )
+            part = pltpu.roll(part, c * SLOT, 1) if c else part
+            total = part if total is None else total + part
+        edge_ref[end] = total
     for store in stores:
         store.wait()
 
@@ -298,14 +346,15 @@
         out_shape=(
             pltpu.HBM(pre, F32),
             pltpu.HBM((rows, operator.shape[0], width - 2 * SIDE), F32),
+            pltpu.HBM((2, rows, 128), F32),
         )
         + tuple(pltpu.HBM(shape, BF16) for shape in slopes),
         in_specs=[smem_spec()] + vmem_specs(6) + far_specs(3),
-        out_specs=tuple(far_specs(1) + vmem_specs(1) + far_specs(3)),
+        out_specs=tuple(far_specs(1) + vmem_specs(2) + far_specs(3)),
         scratch_shapes=[pltpu.VMEM((padded, 3 * LANES), BF16)] * 2
         + [pltpu.VMEM((BLOCK * width, LANES), F32)] * 2
         + weight_scratch(weights)
-        + [pltpu.VMEM(pre, F32)]
+        + [pltpu.VMEM(pre, F32)] + [pltpu.VMEM((rows * width, 128), F32)] * 2
         + [pltpu.VMEM(shape, BF16) for shape in slopes]
         + [pltpu.SemaphoreType.DMA((LAYERS,)), pltpu.SemaphoreType.DMA((LAYERS,))],
         compiler_params=params(34),
@@ -321,13 +370,13 @@
 
 
 def edge_kernel(
-    place_ref, recv_ref, pred_ref, op_ref, prec_ref, d0_far, d1_far, d2_far, w0_far, wm_far, w3_far,
+    place_ref, recv_ref, pred_ref, pred_edge_ref, op_ref, prec_ref, prec_edge_ref,
+    d0_far, d1_far, d2_far, w0_far, wm_far, w3_far,
     pulled_ref, near_ref, far_ref, s0_ref, s1_ref, s2_ref,
-    wide_ref, sums_ref, buf_a, buf_b, acc_a, acc_b, w0, wm, w3, d_ref, in_sems,
+    wide_ref, sums_ref, field_a, field_b, buf_a, buf_b, acc_a, acc_b, w0, wm, w3, d_ref, in_sems,
 ):
-    rows, cells, channels = pulled_ref.shape
+    rows, cells, channels = pred_ref.shape[0], pred_ref.shape[2], near_ref.shape[1]
     width = cells + 2 * SIDE
-    bands = 22
     slots = recv_ref.shape[0] // SLOT
     weights = (w0, wm.at[0], wm.at[1], w3)
     strips = (s0_ref, s1_ref, s2_ref)
@@ -350,23 +399,52 @@
 
     wide_ref[...] = recv_ref[...].astype(F32)
     sums_ref[...] = jnp.zeros(sums_ref.shape, F32)
-    numbers = wide_ref[pl.ds(bands, slots, stride=SLOT), :]
-    lane = lax.broadcasted_iota(jnp.int32, (slots, cells), 1).astype(F32) + 1.0
-    onehot = jnp.transpose((numbers == lane).astype(F32))[0:rows, :].astype(BF16)
+    sides = [wide_ref[pl.ds(BANDS + end, slots, stride=SLOT), :] for end in range(2)]
+    lane = lax.broadcasted_iota(jnp.int32, (slots, cells), 1).astype(F32)
+    own = sides[0][:, BANDS + 1 : BANDS + 2]
+    before = sides[0][:, BANDS : BANDS + 1] + rows
+    after = sides[1][:, BANDS : BANDS + 1] + 2 * rows
+    wanted = jnp.where(lane < rows, own, jnp.where(lane < 2 * rows, before, after))
+    least = jnp.where(lane < rows, 0.0, jnp.where(lane < 2 * rows, 1.0 * rows, 2.0 * rows))
+    match = (wanted == lane + 1.0) & (wanted > least) & (lane < 3 * rows)
+    onehot = jnp.transpose(match.astype(F32))[0 : 3 * rows, :].astype(BF16)
     held = jnp.dot(onehot, jnp.ones((slots, cells), BF16), preferred_element_type=F32)
-    for k in range(bands):
+    own_hot = onehot[0:rows, :]
+    for k in range(BANDS):
         part = wide_ref[pl.ds(k, slots, stride=SLOT), :].astype(BF16)
-        sums_ref[pl.ds(k, rows, stride=32), :] = jnp.dot(onehot, part, preferred_element_type=F32)
+        sums_ref[pl.ds(k, rows, stride=32), :] = jnp.dot(own_hot, part, preferred_element_type=F32)
+    nothing = jnp.zeros((SIDE, 128), F32)
     for r in range(rows):
         summed = sums_ref[r * 32 : (r + 1) * 32, :]
         weighted = (summed - held[r : r + 1, :] * pred_ref[r]) * prec_ref[...]
-        pulled = jnp.dot(
+        at = r * width
+        value = jnp.dot(
             jnp.transpose(weighted).astype(BF16), op_ref[...], preferred_element_type=F32
         )
-        pulled_ref[r] = pulled
+        for field, part in ((field_a, value[:, 0:128]), (field_b, value[:, 128:LANES])):
+            field[at : at + SIDE, :] = nothing
+            field[at + SIDE : at + SIDE + cells, :] = part
+            field[at + SIDE + cells : at + width, :] = nothing
+    short = op_ref[...].astype(F32)[0:SLOT, :]
+    for end, first in ((0, SIDE - EDGE), (1, SIDE + cells)):
+        part = onehot[(1 + end) * rows : (2 + end) * rows, :]
+        summed = jnp.dot(part, sides[end].astype(BF16), preferred_element_type=F32)
+        count = held[(1 + end) * rows : (2 + end) * rows, :]
+        weighted = ((summed - count * pred_edge_ref[end]) * prec_edge_ref[...]).astype(BF16)
+        for c in range(EDGE):
+            above = [jnp.zeros((c * SLOT, LANES), F32)] if c else []
+            below = jnp.zeros((128 - (c + 1) * SLOT, LANES), F32)
+            picked = jnp.concatenate(above + [short, below], axis=0).astype(BF16)
+            value = jnp.dot(weighted, picked, preferred_element_type=F32)
+            at = pl.ds(first + c, rows, stride=width)
+            field_a[at, :] = value[:, 0:128]
+            field_b[at, :] = value[:, 128:LANES]
+    for r in range(rows):
+        at = slice(r * width, (r + 1) * width)
+        row = jnp.concatenate([field_a[at, :], field_b[at, :]], axis=1)[:, 0:channels]
+        pulled_ref[r] = row
         if r < HALO or r >= rows - HALO:
-            side = jnp.zeros((SIDE, channels), F32)
-            put_shifted(buf_a, r + LEAD, width, jnp.concatenate([side, pulled, side], axis=0))
+            put_shifted(buf_a, r + LEAD, width, row)
 
     src, dst = buf_a, buf_b
     for layer in range(LAYERS - 1, -1, -1):
@@ -388,14 +466,17 @@
                 kept = value[half:, :] if end == 0 else value[0:half, :]
                 strips[layer - 1][end * half : (end + 1) * half, :] = kept.astype(BF16)
         else:
-            top = acc_a[:, 0:channels]
-            low = acc_b[:, 0:channels]
-            near_ref[...] = either(place_ref[1], low, top).astype(BF16)
-            far_ref[...] = either(place_ref[1], top, low).astype(BF16)
+            for i in range(HALO):
+                at = slice(i * width + SIDE, i * width + SIDE + cells)
+                top = acc_a[at, 0:channels]
+                low = acc_b[at, 0:channels]
+                out = slice(i * cells, (i + 1) * cells)
+                near_ref[out, :] = either(place_ref[1], low, top).astype(BF16)
+                far_ref[out, :] = either(place_ref[1], top, low).astype(BF16)
         src, dst = dst, src
 
 
-def edge_pass(place, recv, pred, slopes, operator, precision, weights, channels):
+def edge_pass(place, recv, pred, pred_edge, slopes, operator, precision, precision_edge, weights, channels):
     rows, cells = pred.shape[0], pred.shape[2]
     width = cells + 2 * SIDE
     padded = (rows + 2 * LEAD) * width
@@ -403,16 +484,18 @@
     return pl.pallas_call(
         edge_kernel,
         out_shape=(
-            pltpu.HBM((rows, cells, channels), F32),
-            jax.ShapeDtypeStruct((size, channels), BF16),
-            jax.ShapeDtypeStruct((size, channels), BF16),
+            pltpu.HBM((rows, width, channels), F32),
+            jax.ShapeDtypeStruct((HALO * cells, channels), BF16),
+            jax.ShapeDtypeStruct((HALO * cells, channels), BF16),
         )
         + tuple(pltpu.HBM((size, LANES), BF16) for _ in range(LAYERS - 1)),
-        in_specs=[smem_spec()] + vmem_specs(4) + far_specs(6),
+        in_specs=[smem_spec()] + vmem_specs(6) + far_specs(6),
         out_specs=tuple(vmem_specs(6)),
         scratch_shapes=[
             pltpu.VMEM(recv.shape, F32),
             pltpu.VMEM((rows * 32, recv.shape[1]), F32),
+            pltpu.VMEM((rows * width, 128), F32),
+            pltpu.VMEM((rows * width, 128), F32),
         ]
         + [pltpu.VMEM((padded, 3 * LANES), BF16)] * 2
         + [pltpu.VMEM((size, LANES), F32)] * 2
@@ -420,16 +503,17 @@
         + [pltpu.VMEM((LAYERS - 1, 2, size, LANES), BF16), pltpu.SemaphoreType.DMA((LAYERS + 6,))],
         compiler_params=params(34),
         name="edge_pass",
-    )(place, recv, *in_hbm(pred), operator, precision, *in_hbm(*slopes, *weights))
+    )(place, recv, *in_hbm(pred, pred_edge), operator, precision, precision_edge, *in_hbm(*slopes, *weights))
 
 
 def inner_kernel(
-    scale_ref, pulled_ref, s0_ref, s1_ref, s2_ref, pre_far, d0_far, d1_far, d2_far, w0_far, wm_far, w3_far,
+    level_ref, pulled_ref, s0_ref, s1_ref, s2_ref, pre_far, d0_far, d1_far, d2_far, w0_far, wm_far, w3_far,
     own_ref,
     buf_a, buf_b, acc_a, acc_b, w0, wm, w3, pre_ref, d0, d1, d2, in_sems,
 ):
-    rows, cells, channels = pulled_ref.shape
-    width = cells + 2 * SIDE
+    rows, width, _ = pulled_ref.shape
+    cells = width - 2 * SIDE
+    inverse = 1.0 / (level_ref[...] * level_ref[...])
     weights = (w0, wm.at[0], wm.at[1], w3)
     strips = (s0_ref, s1_ref, s2_ref)
     slopes = (d0, d1, d2)
@@ -445,8 +529,7 @@
         load.start()
 
     def fill(r, carry):
-        side = jnp.zeros((SIDE, channels), F32)
-        put_shifted(buf_a, r + LEAD, width, jnp.concatenate([side, pulled_ref[r], side], axis=0))
+        put_shifted(buf_a, r + LEAD, width, pulled_ref[r])
         return carry
 
     lax.fori_loop(0, rows, fill, 0)
@@ -478,24 +561,22 @@
             loads[-1].wait()
 
             def finish(row, n, value):
-                side = jnp.zeros((SIDE, channels), F32)
                 for i in range(n):
-                    base = pre_ref[row + i][SIDE : SIDE + cells, :] * scale_ref[0] + pulled_ref[row + i]
-                    base = jnp.concatenate([side, base, side], axis=0)
-                    own_ref[row + i] = base + value[i * width : (i + 1) * width, :]
+                    total = pre_ref[row + i] * inverse + pulled_ref[row + i] + value[i * width : (i + 1) * width, :]
+                    own_ref[row + i] = total[SIDE : SIDE + cells, :]
 
             conv_layer(count, compute, finish, acc_a, acc_b)
         src, dst = dst, src
 
 
-def inner_pass(scale, pulled, strips, pre, slopes, weights):
+def inner_pass(level, pulled, strips, pre, slopes, weights):
     rows, width, channels = pre.shape
     padded = (rows + 2 * LEAD) * width
     kept = [((rows - 2 * (layer + 1)) * width, LANES) for layer in range(LAYERS - 1)]
     return pl.pallas_call(
         inner_kernel,
-        out_shape=pltpu.HBM((rows, width, channels), F32),
-        in_specs=[smem_spec()] + vmem_specs(4) + far_specs(7),
+        out_shape=pltpu.HBM((rows, width - 2 * SIDE, channels), F32),
+        in_specs=vmem_specs(5) + far_specs(7),
         out_specs=vmem_specs(1)[0],
         scratch_shapes=[pltpu.VMEM((padded, 3 * LANES), BF16)] * 2
         + [pltpu.VMEM((BLOCK * width, LANES), F32)] * 2
@@ -505,39 +586,35 @@
         + [pltpu.SemaphoreType.DMA((2 * LAYERS,))],
         compiler_params=params(34),
         name="inner_pass",
-    )(scale, *in_hbm(pulled, *strips, pre, *slopes, *weights))
-
-
-def final_kernel(
-    scale_ref, own_ref, above_ref, below_ref, left_ref, right_ref, state_ref, noise_ref, out_ref
-):
-    rows, width = own_ref.shape[0], own_ref.shape[1]
-    cells = width - 2 * SIDE
+    )(level, *in_hbm(pulled, *strips, pre, *slopes, *weights))
+
+
+def final_kernel(place_ref, step_ref, own_ref, near_ref, far_ref, state_ref, noise_ref, out_ref):
+    rows, cells = own_ref.shape[0], own_ref.shape[1]
+    step = step_ref[...]
+    spread = jnp.sqrt(2.0 * step)
     for r in range(rows):
-        total = own_ref[r][SIDE : SIDE + cells, :]
-        if r < HALO:
-            total = total + above_ref[r * width : (r + 1) * width, :].astype(F32)[SIDE : SIDE + cells, :]
-        if r >= rows - HALO:
-            at = r - (rows - HALO)
-            total = total + below_ref[at * width : (at + 1) * width, :].astype(F32)[SIDE : SIDE + cells, :]
-        first = total[0:SIDE, :] + left_ref[r]
-        last = total[cells - SIDE : cells, :] + right_ref[r]
-        total = jnp.concatenate([first, total[SIDE : cells - SIDE, :], last], axis=0)
-        turned = jnp.transpose(total)
-        out_ref[:, r, :] = (
-            state_ref[:, r, :] + scale_ref[0] * turned + scale_ref[1] * noise_ref[:, r, :]
-        )
-
-
-def final_pass(scale, own, above, below, left, right, state, noise):
+        total = own_ref[r]
+        at = r if r < HALO else r - (rows - HALO)
+        if r < HALO or r >= rows - HALO:
+            near = near_ref[at * cells : (at + 1) * cells, :].astype(F32)
+            far = far_ref[at * cells : (at + 1) * cells, :].astype(F32)
+            if r < HALO:
+                total = total + either(place_ref[1], far, near)
+            else:
+                total = total + either(place_ref[1], near, far)
+        out_ref[:, r, :] = state_ref[:, r, :] + step * jnp.transpose(total) + spread * noise_ref[:, r, :]
+
+
+def final_pass(place, step, own, near, far, state, noise):
     return pl.pallas_call(
         final_kernel,
         out_shape=jax.ShapeDtypeStruct(state.shape, F32),
-        in_specs=[smem_spec()] + vmem_specs(7),
+        in_specs=[smem_spec()] + vmem_specs(6),
         out_specs=vmem_specs(1)[0],
         compiler_params=params(16),
         name="final_pass",
-    )(scale, *in_hbm(own), above, below, left, right, *near_core(state, noise))
+    )(place, step, *in_hbm(own), near, far, *near_core(state, noise))
 
 
 def swap_pairs(size, first, wrap):
@@ -551,12 +628,6 @@
 def swap(axis, wrap, near, far):
     size = lax.axis_size(axis)
     return lax.ppermute(near, axis, swap_pairs(size, 0, wrap)), lax.ppermute(far, axis, swap_pairs(size, 1, wrap))
-
-
-def exchange(axis, wrap, to_before, to_after):
-    even = lax.axis_index(axis) % 2 == 0
-    near, far = swap(axis, wrap, jnp.where(even, to_after, to_before), jnp.where(even, to_before, to_after))
-    return jnp.where(even, far, near), jnp.where(even, near, far)
 
 
 def pad_to(values, shape):
@@ -584,14 +655,8 @@
     bands = lax.axis_size("lat")
     place = jnp.stack([lon % 2 == 0, lat % 2 == 0, lat == 0, lat == bands - 1]).astype(jnp.int32)
 
-    targets = obs_holder[:, 0]
-    count = targets.shape[0]
-    positions = lax.broadcasted_iota(jnp.int32, (count, count), 0)
-    earlier = lax.broadcasted_iota(jnp.int32, (count, count), 1)
-    before = (targets[:, None] == targets[None, :]) & (earlier < positions)
-    slots = targets * CAPACITY + jnp.sum(before.astype(jnp.int32), axis=1)
     holders = lax.axis_size(("lon", "lat"))
-    packed = pack_blocks(slots, obs_tile, obs_values, holders * CAPACITY)
+    packed = pack_blocks(obs_holder, obs_tile, obs_values, holders * CAPACITY, bands * CAPACITY)
     own, *edges = turn_state(place, state)
     lon_halo = swap("lon", True, *edges)
     framed = frame_rows(place, own, *lon_halo, width)
@@ -601,31 +666,16 @@
         packed.reshape(holders, CAPACITY * SLOT, cells), ("lon", "lat"), split_axis=0, concat_axis=0, tiled=True
     ).reshape(packed.shape)
 
-    operator = pad_to(obs_operator, (32, channels))
+    operator = pad_to(obs_operator, (32, LANES))
     precision = pad_to(obs_precision[:, None], (32, 1))
-    pre, pred, *slopes = forward_pass(place, own, lon_halo, lat_halo, weights, operator, rows, width)
-    inverse = (1.0 / (noise_level * noise_level)).astype(F32)
+    precision_edge = pad_to(jnp.tile(pad_to(obs_precision, (SLOT,)), EDGE)[None, :], (1, 128))
+    pre, pred, pred_edge, *slopes = forward_pass(place, own, lon_halo, lat_halo, weights, operator, rows, width)
     pulled, near, far, *strips = edge_pass(
-        place, recv, pred, slopes, operator, precision, weights, channels
+        place, recv, pred, pred_edge, slopes, operator, precision, precision_edge, weights, channels
     )
     near, far = swap("lat", False, near, far)
-    own = inner_pass(inverse, pulled, strips, pre, slopes, weights)
-    even = place[1] == 1
-    above, below = jnp.where(even, far, near), jnp.where(even, near, far)
-    above_side = above.reshape(HALO, width, channels)
-    below_side = below.reshape(HALO, width, channels)
-
-    def edge(at):
-        added = [
-            above_side[:, at : at + SIDE].astype(F32),
-            jnp.zeros((rows - 2 * HALO, SIDE, channels), F32),
-            below_side[:, at : at + SIDE].astype(F32),
-        ]
-        return (own[:, at : at + SIDE] + jnp.concatenate(added, axis=0)).astype(BF16)
-
-    left, right = exchange("lon", True, edge(0), edge(width - SIDE))
-    scale = jnp.stack([step_size[0], jnp.sqrt(2.0 * step_size[0])])
-    return final_pass(scale, own, above, below, left.astype(F32), right.astype(F32), state, noise)
+    own = inner_pass(noise_level.reshape(1, 1), pulled, strips, pre, slopes, weights)
+    return final_pass(place, step_size.reshape(1, 1), own, near, far, state, noise)
 
 
 def solution(mesh):

time: 127 us -> 119 us (0.937)
  starting transfers between devices: 27.5 us -> 24.3 us
  other arithmetic: 2.97 us -> 0.08 us
  waiting for transfers between devices: 28.9 us -> 26.7 us
  Pallas kernels: 61.5 us -> 63 us
    ppermute x4 -> x3, starting transfers between devices: 17.6 us -> 13.8 us  [swap(): lax.ppermute(far, axis, swap_pairs(size, 1, wrap))]
    ppermute x4 -> x3, waiting for transfers between devices: 2.08 us -> 0.01 us  [swap(): lax.ppermute(far, axis, swap_pairs(size, 1, wrap))]
    pallas_call x3, Pallas kernels: 29.1 us -> 30.7 us  [the longest x1 16.5 us: inner_pass(): pl.pallas_call(inner_kernel, out_shape=pltpu.HBM((rows, width - 2 * SIDE,...]
    unnamed x12 -> x16, local copies, waits for them, and re-layouts: 1.37 us -> 2.68 us
    ppermute x4 -> x3, waiting for transfers between devices: 26.8 us -> 26.7 us  [swap(): lax.ppermute(near, axis, swap_pairs(size, 0, wrap))]
    ppermute x4 -> x3, starting transfers between devices: 3.25 us -> 3.17 us  [swap(): lax.ppermute(near, axis, swap_pairs(size, 0, wrap))]
  transfers between devices with their start and end apart: 9 -> 7, of which waited for: 2 -> 1; matrix products, arithmetic and copies ran while one was open for 3% -> 0% of each run, Pallas kernels for 33% -> 36%
where the time goes in v2:
time: 119 us; the launch traced here: 118 us
  Pallas kernels  63 us (53%)
  waiting for transfers between devices  26.7 us (22%)
  starting transfers between devices  24.3 us (20%)
  local copies, waits for them, and re-layouts  2.89 us (2%)
  between operations  1.47 us (1%)
    ppermute x3, waiting for transfers between devices, swap(): lax.ppermute(near, axis, swap_pairs(size, 0, wrap))  26.7 us
    pallas_call x1, Pallas kernels, forward_pass(): pl.pallas_call(forward_kernel, out_shape=(pltpu.HBM(pre, F32), pltpu.HBM(...  23.4 us
    pallas_call x1, Pallas kernels, inner_pass(): pl.pallas_call(inner_kernel, out_shape=pltpu.HBM((rows, width - 2 * SIDE,...  16.5 us
    ppermute x3, starting transfers between devices, swap(): lax.ppermute(far, axis, swap_pairs(size, 1, wrap))  13.8 us
    pallas_call x1, Pallas kernels, edge_pass(): pl.pallas_call(edge_kernel, out_shape=(pltpu.HBM((rows, width, channels),...  11.8 us
    all_to_all x1, starting transfers between devices, shards(): lax.all_to_all(packed.reshape(holders, CAPACITY * SLOT, cells), ('lon', '...  7.29 us
    pallas_call x1, Pallas kernels, final_pass(): pl.pallas_call(final_kernel, out_shape=jax.ShapeDtypeStruct(state.shape,...  5.17 us
    ppermute x3, starting transfers between devices, swap(): lax.ppermute(near, axis, swap_pairs(size, 0, wrap))  3.17 us
  transfers between devices with their start and end apart: 7, of which 1 were waited for; matrix products, arithmetic and copies ran while one was open for 0% of the time, Pallas kernels for 36%

profile of v2, /device:TPU:6, one launch (start us, length us, event | category | flops | bytes accessed | tf_op | source)
XLA Modules:
  0.0 118.5 jit_solution(5053046205102679119)
XLA Ops:
  0.0 0.1 add_convert_fusion.place_ref
  0.1 1.3 %copy-done = f32[168,16,128]{2,1,0:T(8,128)S(1)} copy-done((f32[168,16,128]{2,1,0:T(8,128)S(1)}, f32[168,16,128]{2,1,0:T(8,128)}, u32[]{:S(2)}) %copy-start) | copy-done | bytes 1376280
  1.4 2.3 %turn_state.1 = (bf16[2048,168]{1,0:T(8,128)(2,1)}, bf16[128,168]{1,0:T(8,128)(2,1)S(1)}, bf16[128,168]{1,0:T(8,128)(2,1)S(1)}) custom-call(s32[4]{0:T(128)S(1)} %add_convert_fusion.place_ref, f32[168,16,128]{2,1,0:T(8,128)S(1)} %copy-done), custom_call_target="tpu_custom_call" | custom-call | tf_op jit(solution)/shard_map/turn_state/pallas_call | solution.py:189
  3.7 0.0 collective-permute-start
  3.7 5.2 %collective-permute-start.1 = (bf16[128,168]{1,0:T(8,128)(2,1)S(1)}, bf16[128,168]{1,0:T(8,128)(2,1)S(1)}, u32[]{:S(2)}, u32[]{:S(2)}) collective-permute-start(bf16[128,168]{1,0:T(8,128)(2,1)S(1)} %get-tuple-element.27), channel_id=1, source_target_pairs={{8,16},{16,8},{24,32},{32,24},{40,48},{48,40},{56,64},{64,56},{72,... | collective-permute-start | bytes 129032 | tf_op jit(solution)/shard_map/ppermute | solution.py:630
  8.9 0.0 copy-done.3
  8.9 0.7 copy-done.4
  9.6 0.7 copy-done.5
  10.2 2.4 %pack_blocks.1 = bf16[6144,128]{1,0:T(8,128)(2,1)} custom-call(s32[1,96]{1,0:T(1,128)S(1)} %bitcast.17, s32[1,96]{1,0:T(1,128)S(1)} %bitcast.18, bf16[22,96,128]{2,1,0:T(8,128)(2,1)S(1)} %bitcast.16), custom_call_target="tpu_custom_call" | custom-call | tf_op jit(solution)/shard_map/pack_blocks/pallas_call | solution.py:96
  12.6 0.0 collective-permute-done.lon_near_ref
  12.7 0.0 collective-permute-done.1.lon_far_ref
  12.7 1.4 %frame_rows.1 = (bf16[576,168]{1,0:T(8,128)(2,1)S(1)}, bf16[576,168]{1,0:T(8,128)(2,1)S(1)}) custom-call(s32[4]{0:T(128)S(1)} %add_convert_fusion.place_ref, bf16[2048,168]{1,0:T(8,128)(2,1)} %get-tuple-element.25.own_ref, bf16[128,168]{1,0:T(8,128)(2,1)S(1)} %collective-permute-done.lon_near_ref, bf16[128,168]{1,0:T(8,128)(2,1)S(1)} %collective-permute-done.1.lon_far_ref), custom_call_target="tpu_custom_call" | custom-call | tf_op jit(solution)/shard_map/frame_rows/pallas_call | solution.py:228
  14.0 0.0 copy-start.7
  14.0 0.0 copy-start.6
  14.1 7.3 %all-to-all-start = ((bf16[128,48,128]{2,1,0:T(8,128)(2,1)}), bf16[128,48,128]{2,1,0:T(8,128)(2,1)S(1)}, u32[]{:S(2)}, u32[]{:S(2)}) async-start(bf16[128,48,128]{2,1,0:T(8,128)(2,1)} %bitcast.9), calls=%async_computation | async-start | bytes 3145728 | tf_op jit(solution)/shard_map/all_to_all | solution.py:665
  21.4 3.1 %collective-permute-start.2 = (bf16[576,168]{1,0:T(8,128)(2,1)S(1)}, bf16[576,168]{1,0:T(8,128)(2,1)S(1)}, u32[]{:S(2)}, u32[]{:S(2)}) collective-permute-start(bf16[576,168]{1,0:T(8,128)(2,1)S(1)} %get-tuple-element.31), channel_id=1, source_target_pairs={{0,1},{1,0},{2,3},{3,2},{4,5},{5,4},{6,7},{7,6},{8,9},{9,8},{10,11... | collective-permute-start | bytes 580616 | tf_op jit(solution)/shard_map/ppermute | solution.py:630
  24.4 2.7 %collective-permute-start.3 = (bf16[576,168]{1,0:T(8,128)(2,1)S(1)}, bf16[576,168]{1,0:T(8,128)(2,1)S(1)}, u32[]{:S(2)}, u32[]{:S(2)}) collective-permute-start(bf16[576,168]{1,0:T(8,128)(2,1)S(1)} %get-tuple-element.32), channel_id=1, source_target_pairs={{1,2},{2,1},{3,4},{4,3},{5,6},{6,5},{9,10},{10,9},{11,12},{12,11},... | collective-permute-start | bytes 580616 | tf_op jit(solution)/shard_map/ppermute | solution.py:630
  27.2 0.1 copy.13
  27.3 0.1 broadcast_in_dim_tile.3
  27.4 26.7 %collective-permute-done.2.lat_near_ref = bf16[576,168]{1,0:T(8,128)(2,1)S(1)} collective-permute-done((bf16[576,168]{1,0:T(8,128)(2,1)S(1)}, bf16[576,168]{1,0:T(8,128)(2,1)S(1)}, u32[]{:S(2)}, u32[]{:S(2)}) %collective-permute-start.2) | collective-permute-done | bytes 193568 | tf_op jit(solution)/shard_map/ppermute | solution.py:630
  54.1 0.0 collective-permute-done.3.lat_far_ref
  54.1 23.4 %forward_pass.1 = (f32[16,144,168]{2,1,0:T(8,128)}, f32[16,32,128]{2,1,0:T(8,128)}, f32[2,16,128]{2,1,0:T(8,128)}, bf16[3168,256]{1,0:T(8,128)(2,1)}, bf16[2880,...) custom-call(s32[4]{0:T(128)S(1)} %add_convert_fusion.place_ref, bf16[2048,168]{1,0:T(8,128)(2,1)} %get-tuple-element.25.own_ref, ...), custom_call_target="tpu_custom_call" | custom-call | tf_op jit(solution)/shard_map/forward_pass/pallas_call | solution.py:344
  77.6 0.0 all-to-all-done
  77.6 11.8 %edge_pass.1 = (f32[16,144,168]{2,1,0:T(8,128)}, bf16[512,168]{1,0:T(8,128)(2,1)S(1)}, bf16[512,168]{1,0:T(8,128)(2,1)S(1)}, bf16[576,256]{1,0:T(8,128)(2,1)}, b...) custom-call(s32[4]{0:T(128)S(1)} %add_convert_fusion.place_ref, bf16[6144,128]{1,0:T(8,128)(2,1)S(1)} %bitcast.15, ...), custom_call_target="tpu_custom_call" | custom-call | tf_op jit(solution)/shard_map/edge_pass/pallas_call | solution.py:484
  89.4 0.1 collective-permute-start.4
  89.5 6.0 %collective-permute-start.5 = (bf16[512,168]{1,0:T(8,128)(2,1)S(1)}, bf16[512,168]{1,0:T(8,128)(2,1)S(1)}, u32[]{:S(2)}, u32[]{:S(2)}) collective-permute-start(bf16[512,168]{1,0:T(8,128)(2,1)S(1)} %get-tuple-element.44), channel_id=1, source_target_pairs={{1,2},{2,1},{3,4},{4,3},{5,6},{6,5},{9,10},{10,9},{11,12},{12,11},... | collective-permute-start | bytes 516104 | tf_op jit(solution)/shard_map/ppermute | solution.py:630
  96.7 0.0 copy-start.1
  96.7 0.0 copy-start.2
  96.8 16.5 %inner_pass.1.own_ref = f32[16,128,168]{2,1,0:T(8,128)} custom-call(f32[1,1]{1,0:T(1,128)} %bitcast.13.level_ref, f32[16,144,168]{2,1,0:T(8,128)} %get-tuple-element.38.pulled_ref, bf16[576,256]{1,0:T(8,128)(2,1)} %get-tuple-element.39.s0_ref, bf16[576,256]{1,0:T(8,128)(2,1)} %get-tuple-element.40.s1_ref, bf16[576,256]{1,0:T(8,128)(2,1)} %get-tuple-element.41.s2_ref, ...), custom_call_target="tpu_custom_call" | custom-call | tf_op jit(solution)/shard_map/inner_pass/pallas_call | solution.py:576
  113.2 0.0 collective-permute-done.4.near_ref
  113.3 0.0 collective-permute-done.5.far_ref
  113.3 5.2 %final_pass.1 = f32[168,16,128]{2,1,0:T(8,128)} custom-call(s32[4]{0:T(128)S(1)} %add_convert_fusion.place_ref, f32[1,1]{1,0:T(1,128)} %bitcast.14.step_ref, f32[16,128,168]{2,1,0:T(8,128)} %inner_pass.1.own_ref, bf16[512,168]{1,0:T(8,128)(2,1)S(1)} %collective-permute-done.4.near_ref, bf16[512,168]{1,0:T(8,128)(2,1)S(1)} %collective-permute-done.5.far_ref, ...), custom_call_target="tpu_custom_call" | custom-call | tf_op jit(solution)/shard_map/final_pass/pallas_call | solution.py:610
  (13 shorter events, 0.0 us)
Async XLA Ops:
  0.1 1.3 %copy-start = (f32[168,16,128]{2,1,0:T(8,128)S(1)}, f32[168,16,128]{2,1,0:T(8,128)}, u32[]{:S(2)}) copy-start(f32[168,16,128]{2,1,0:T(8,128)} %state_ref.3) | copy-start | bytes 4128772
  1.4 7.5 %copy-start.3 = (bf16[96,22,128]{2,0,1:T(8,128)(2,1)S(1)}, bf16[96,22,128]{2,0,1:T(8,128)(2,1)}, u32[]{:S(2)}) copy-start(bf16[96,22,128]{2,0,1:T(8,128)(2,1)} %param.17) | copy-start | bytes 1622020
  3.7 8.9 %collective-permute-start = (bf16[128,168]{1,0:T(8,128)(2,1)S(1)}, bf16[128,168]{1,0:T(8,128)(2,1)S(1)}, u32[]{:S(2)}, u32[]{:S(2)}) collective-permute-start(bf16[128,168]{1,0:T(8,128)(2,1)S(1)} %get-tuple-element.26), channel_id=1, source_target_pairs={{0,8},{8,0},{16,24},{24,16},{32,40},{40,32},{48,56},{56,48},{64,72... | collective-permute-start | bytes 129032 | tf_op jit(solution)/shard_map/ppermute | solution.py:630
  3.7 8.9 %collective-permute-start.1 = (bf16[128,168]{1,0:T(8,128)(2,1)S(1)}, bf16[128,168]{1,0:T(8,128)(2,1)S(1)}, u32[]{:S(2)}, u32[]{:S(2)}) collective-permute-start(bf16[128,168]{1,0:T(8,128)(2,1)S(1)} %get-tuple-element.27), channel_id=1, source_target_pairs={{8,16},{16,8},{24,32},{32,24},{40,48},{48,40},{56,64},{64,56},{72,... | collective-permute-start | bytes 129032 | tf_op jit(solution)/shard_map/ppermute | solution.py:630
  8.9 0.7 copy-start.4
  9.6 0.7 copy-start.5
  14.0 13.1 %copy-start.7 = (f32[22]{0:T(128)S(1)}, f32[22]{0:T(128)}, u32[]{:S(2)}) copy-start(f32[22]{0:T(128)} %param.21) | copy-start | bytes 268
  14.0 13.3 %copy-start.6 = (bf16[22,168]{1,0:T(8,128)(2,1)S(1)}, bf16[22,168]{1,0:T(8,128)(2,1)}, u32[]{:S(2)}) copy-start(bf16[22,168]{1,0:T(8,128)(2,1)} %param.20) | copy-start | bytes 22180
  14.1 63.5 %all-to-all-start = ((bf16[128,48,128]{2,1,0:T(8,128)(2,1)}), bf16[128,48,128]{2,1,0:T(8,128)(2,1)S(1)}, u32[]{:S(2)}, u32[]{:S(2)}) async-start(bf16[128,48,128]{2,1,0:T(8,128)(2,1)} %bitcast.9), calls=%async_computation | async-start | bytes 3145728 | tf_op jit(solution)/shard_map/all_to_all | solution.py:665
  21.4 32.8 %collective-permute-start.2 = (bf16[576,168]{1,0:T(8,128)(2,1)S(1)}, bf16[576,168]{1,0:T(8,128)(2,1)S(1)}, u32[]{:S(2)}, u32[]{:S(2)}) collective-permute-start(bf16[576,168]{1,0:T(8,128)(2,1)S(1)} %get-tuple-element.31), channel_id=1, source_target_pairs={{0,1},{1,0},{2,3},{3,2},{4,5},{5,4},{6,7},{7,6},{8,9},{9,8},{10,11... | collective-permute-start | bytes 580616 | tf_op jit(solution)/shard_map/ppermute | solution.py:630
  24.4 29.7 %collective-permute-start.3 = (bf16[576,168]{1,0:T(8,128)(2,1)S(1)}, bf16[576,168]{1,0:T(8,128)(2,1)S(1)}, u32[]{:S(2)}, u32[]{:S(2)}) collective-permute-start(bf16[576,168]{1,0:T(8,128)(2,1)S(1)} %get-tuple-element.32), channel_id=1, source_target_pairs={{1,2},{2,1},{3,4},{4,3},{5,6},{6,5},{9,10},{10,9},{11,12},{12,11},... | collective-permute-start | bytes 580616 | tf_op jit(solution)/shard_map/ppermute | solution.py:630
  89.4 23.9 %collective-permute-start.4 = (bf16[512,168]{1,0:T(8,128)(2,1)S(1)}, bf16[512,168]{1,0:T(8,128)(2,1)S(1)}, u32[]{:S(2)}, u32[]{:S(2)}) collective-permute-start(bf16[512,168]{1,0:T(8,128)(2,1)S(1)} %get-tuple-element.43), channel_id=1, source_target_pairs={{0,1},{1,0},{2,3},{3,2},{4,5},{5,4},{6,7},{7,6},{8,9},{9,8},{10,11... | collective-permute-start | bytes 516104 | tf_op jit(solution)/shard_map/ppermute | solution.py:630
  89.5 23.8 %collective-permute-start.5 = (bf16[512,168]{1,0:T(8,128)(2,1)S(1)}, bf16[512,168]{1,0:T(8,128)(2,1)S(1)}, u32[]{:S(2)}, u32[]{:S(2)}) collective-permute-start(bf16[512,168]{1,0:T(8,128)(2,1)S(1)} %get-tuple-element.44), channel_id=1, source_target_pairs={{1,2},{2,1},{3,4},{4,3},{5,6},{6,5},{9,10},{10,9},{11,12},{12,11},... | collective-permute-start | bytes 516104 | tf_op jit(solution)/shard_map/ppermute | solution.py:630
  96.7 16.5 %copy-start.1 = (f32[168,16,128]{2,1,0:T(8,128)S(1)}, f32[168,16,128]{2,1,0:T(8,128)}, u32[]{:S(2)}) copy-start(f32[168,16,128]{2,1,0:T(8,128)} %state_ref.3) | copy-start | bytes 4128772
  96.7 16.5 %copy-start.2 = (f32[168,16,128]{2,1,0:T(8,128)S(1)}, f32[168,16,128]{2,1,0:T(8,128)}, u32[]{:S(2)}) copy-start(f32[168,16,128]{2,1,0:T(8,128)} %noise_ref.1) | copy-start | bytes 4128772

commit v3 on v2

--- a/solution.py
+++ b/solution.py
@@ -29,10 +29,6 @@
 
 def params(mebibytes):
     return pltpu.CompilerParams(vmem_limit_bytes=mebibytes << 20)
-
-
-def near_core(*arrays):
-    return [pltpu.with_memory_space_constraint(array, pltpu.VMEM) for array in arrays]
 
 
 def in_hbm(*arrays):
@@ -101,7 +97,7 @@
         scratch_shapes=[pltpu.VMEM((slot_count * SLOT, width), F32)],
         compiler_params=params(12),
         name="pack_blocks",
-    )(holders.reshape(1, -1), tiles.reshape(1, -1), jnp.transpose(values, (1, 0, 2)))
+    )(*in_hbm(holders.reshape(1, -1), tiles.reshape(1, -1), jnp.transpose(values, (1, 0, 2))))
 
 
 def put_shifted(dst_ref, row, width, act):
@@ -152,7 +148,10 @@
         finish(row + BLOCK, BLOCK, kept(acc_b, BLOCK))
         return carry
 
-    lax.fori_loop(0, pairs, body, 0)
+    if pairs > 1:
+        lax.fori_loop(0, pairs, body, 0)
+    elif pairs:
+        body(0, 0)
     done = 2 * pairs
     last, free = acc_a, acc_b
     if full - 1 > done:
@@ -170,17 +169,34 @@
     return jnp.where(flag == 1, yes, no)
 
 
-def turn_kernel(place_ref, state_ref, own_ref, near_ref, far_ref, low_ref, high_ref):
+def turn_kernel(
+    place_ref, state_far, own_ref, outer_ref, near_ref, far_ref, state_ref, low_ref, high_ref, sems
+):
     _, rows, cells = state_ref.shape
+    half = rows // 2
+    parts = [pl.ds(0, half), pl.ds(half, half)]
+    loads = copies([(state_far.at[:, at, :], state_ref.at[:, at, :]) for at in parts], sems)
+    for load in loads:
+        load.start()
     for r in range(rows):
+        if r % half == 0:
+            loads[r // half].wait()
         part = jnp.transpose(state_ref[:, r, :])
-        own_ref[r * cells : (r + 1) * cells, :] = part.astype(BF16)
+        turned = part.astype(BF16)
+        own_ref[r * cells : (r + 1) * cells, :] = turned
+        if r < HALO or r >= rows - HALO:
+            at = outer_row(r, rows) * cells
+            outer_ref[at : at + cells, :] = turned
         low_ref[r * SIDE : (r + 1) * SIDE, :] = part[0:SIDE, :]
         high_ref[r * SIDE : (r + 1) * SIDE, :] = part[cells - SIDE : cells, :]
     low = low_ref[...]
     high = high_ref[...]
     near_ref[...] = either(place_ref[0], high, low).astype(BF16)
     far_ref[...] = either(place_ref[0], low, high).astype(BF16)
+
+
+def outer_row(r, rows):
+    return r if r < HALO else r - (rows - HALO) + HALO
 
 
 def turn_state(place, state):
@@ -190,22 +206,25 @@
         turn_kernel,
         out_shape=(
             pltpu.HBM((rows * cells, channels), BF16),
+            jax.ShapeDtypeStruct((2 * HALO * cells, channels), BF16),
             jax.ShapeDtypeStruct(edge, BF16),
             jax.ShapeDtypeStruct(edge, BF16),
         ),
-        in_specs=[smem_spec()] + vmem_specs(1),
-        out_specs=tuple(vmem_specs(3)),
-        scratch_shapes=[pltpu.VMEM(edge, F32)] * 2,
+        in_specs=[smem_spec()] + far_specs(1),
+        out_specs=tuple(vmem_specs(4)),
+        scratch_shapes=[pltpu.VMEM(state.shape, F32)]
+        + [pltpu.VMEM(edge, F32)] * 2
+        + [pltpu.SemaphoreType.DMA((2,))],
         compiler_params=params(8),
         name="turn_state",
-    )(place, *near_core(state))
-
-
-def framed_row(place_ref, own_ref, near_ref, far_ref, r, cells):
+    )(place, *in_hbm(state))
+
+
+def framed_row(place_ref, own_ref, near_ref, far_ref, r, cells, held=None):
     at = pl.ds(r * SIDE, SIDE)
     near = near_ref[at, :].astype(F32)
     far = far_ref[at, :].astype(F32)
-    own = own_ref[pl.ds(r * cells, cells), :].astype(F32)
+    own = own_ref[pl.ds((r if held is None else held) * cells, cells), :].astype(F32)
     left = either(place_ref[0], far, near)
     right = either(place_ref[0], near, far)
     return jnp.concatenate([left, own, right], axis=0)
@@ -213,11 +232,11 @@
 
 def frame_kernel(place_ref, own_ref, lon_near_ref, lon_far_ref, near_ref, far_ref):
     rows = lon_near_ref.shape[0] // SIDE
-    cells = own_ref.shape[0] // rows
+    cells = own_ref.shape[0] // (2 * HALO)
     width = cells + 2 * SIDE
     for i in range(HALO):
-        top = framed_row(place_ref, own_ref, lon_near_ref, lon_far_ref, i, cells)
-        low = framed_row(place_ref, own_ref, lon_near_ref, lon_far_ref, rows - HALO + i, cells)
+        top = framed_row(place_ref, own_ref, lon_near_ref, lon_far_ref, i, cells, i)
+        low = framed_row(place_ref, own_ref, lon_near_ref, lon_far_ref, rows - HALO + i, cells, HALO + i)
         at = pl.ds(i * width, width)
         near_ref[at, :] = either(place_ref[1], low, top).astype(BF16)
         far_ref[at, :] = either(place_ref[1], top, low).astype(BF16)
@@ -232,7 +251,7 @@
         out_specs=tuple(vmem_specs(2)),
         compiler_params=params(8),
         name="frame_rows",
-    )(place, *in_hbm(own), lon_near, lon_far)
+    )(place, own, lon_near, lon_far)
 
 
 def weight_scratch(weights):
@@ -470,9 +489,8 @@
                 at = slice(i * width + SIDE, i * width + SIDE + cells)
                 top = acc_a[at, 0:channels]
                 low = acc_b[at, 0:channels]
-                out = slice(i * cells, (i + 1) * cells)
-                near_ref[out, :] = either(place_ref[1], low, top).astype(BF16)
-                far_ref[out, :] = either(place_ref[1], top, low).astype(BF16)
+                near_ref[i] = jnp.transpose(either(place_ref[1], low, top)).astype(BF16)
+                far_ref[i] = jnp.transpose(either(place_ref[1], top, low)).astype(BF16)
         src, dst = dst, src
 
 
@@ -485,8 +503,8 @@
         edge_kernel,
         out_shape=(
             pltpu.HBM((rows, width, channels), F32),
-            jax.ShapeDtypeStruct((HALO * cells, channels), BF16),
-            jax.ShapeDtypeStruct((HALO * cells, channels), BF16),
+            jax.ShapeDtypeStruct((HALO, channels, cells), BF16),
+            jax.ShapeDtypeStruct((HALO, channels, cells), BF16),
         )
         + tuple(pltpu.HBM((size, LANES), BF16) for _ in range(LAYERS - 1)),
         in_specs=[smem_spec()] + vmem_specs(6) + far_specs(6),
@@ -507,13 +525,17 @@
 
 
 def inner_kernel(
-    level_ref, pulled_ref, s0_ref, s1_ref, s2_ref, pre_far, d0_far, d1_far, d2_far, w0_far, wm_far, w3_far,
-    own_ref,
-    buf_a, buf_b, acc_a, acc_b, w0, wm, w3, pre_ref, d0, d1, d2, in_sems,
+    level_ref, step_ref, pulled_ref, s0_ref, s1_ref, s2_ref,
+    pre_far, d0_far, d1_far, d2_far, w0_far, wm_far, w3_far, state_far, noise_far,
+    base_ref,
+    buf_a, buf_b, acc_a, acc_b, w0, wm, w3, pre_ref, d0, d1, d2, state_ref, noise_ref, in_sems,
 ):
     rows, width, _ = pulled_ref.shape
     cells = width - 2 * SIDE
-    inverse = 1.0 / (level_ref[...] * level_ref[...])
+    level = jnp.full((1, 128), level_ref[0], F32)
+    inverse = (1.0 / (level * level))[:, 0:1]
+    step = jnp.full((1, 128), step_ref[0], F32)
+    spread = jnp.sqrt(2.0 * step)
     weights = (w0, wm.at[0], wm.at[1], w3)
     strips = (s0_ref, s1_ref, s2_ref)
     slopes = (d0, d1, d2)
@@ -523,7 +545,7 @@
         count = slopes[layer].shape[0]
         pairs.append((source.at[pl.ds(slope_rows(layer, first) * width, count)], slopes[layer]))
         pairs.append((w0_far, w0) if weight is None else (wm_far.at[weight], wm.at[weight]))
-    pairs.append((pre_far, pre_ref))
+    pairs += [(pre_far, pre_ref), (state_far, state_ref), (noise_far, noise_ref)]
     loads = copies(pairs, in_sems)
     for load in loads:
         load.start()
@@ -558,63 +580,62 @@
             conv_layer(count, compute, finish, acc_a, acc_b)
             loads[2 * (LAYERS - 1 - layer) + 2].wait()
         else:
-            loads[-1].wait()
+            for load in loads[-3:]:
+                load.wait()
 
             def finish(row, n, value):
                 for i in range(n):
                     total = pre_ref[row + i] * inverse + pulled_ref[row + i] + value[i * width : (i + 1) * width, :]
-                    own_ref[row + i] = total[SIDE : SIDE + cells, :]
+                    turned = jnp.transpose(total[SIDE : SIDE + cells, :])
+                    r = row + i
+                    base_ref[:, r, :] = state_ref[:, r, :] + step * turned + spread * noise_ref[:, r, :]
 
             conv_layer(count, compute, finish, acc_a, acc_b)
         src, dst = dst, src
 
 
-def inner_pass(level, pulled, strips, pre, slopes, weights):
-    rows, width, channels = pre.shape
+def inner_pass(level, step, pulled, strips, pre, slopes, weights, state, noise):
+    rows, width, _ = pre.shape
     padded = (rows + 2 * LEAD) * width
     kept = [((rows - 2 * (layer + 1)) * width, LANES) for layer in range(LAYERS - 1)]
     return pl.pallas_call(
         inner_kernel,
-        out_shape=pltpu.HBM((rows, width - 2 * SIDE, channels), F32),
-        in_specs=vmem_specs(5) + far_specs(7),
+        out_shape=jax.ShapeDtypeStruct(state.shape, F32),
+        in_specs=[smem_spec(), smem_spec()] + vmem_specs(4) + far_specs(9),
         out_specs=vmem_specs(1)[0],
         scratch_shapes=[pltpu.VMEM((padded, 3 * LANES), BF16)] * 2
         + [pltpu.VMEM((BLOCK * width, LANES), F32)] * 2
         + weight_scratch(weights)
         + [pltpu.VMEM(pre.shape, F32)]
         + [pltpu.VMEM(shape, BF16) for shape in kept]
-        + [pltpu.SemaphoreType.DMA((2 * LAYERS,))],
+        + [pltpu.VMEM(state.shape, F32)] * 2
+        + [pltpu.SemaphoreType.DMA((2 * LAYERS + 2,))],
         compiler_params=params(34),
         name="inner_pass",
-    )(level, *in_hbm(pulled, *strips, pre, *slopes, *weights))
-
-
-def final_kernel(place_ref, step_ref, own_ref, near_ref, far_ref, state_ref, noise_ref, out_ref):
-    rows, cells = own_ref.shape[0], own_ref.shape[1]
-    step = step_ref[...]
-    spread = jnp.sqrt(2.0 * step)
-    for r in range(rows):
-        total = own_ref[r]
-        at = r if r < HALO else r - (rows - HALO)
-        if r < HALO or r >= rows - HALO:
-            near = near_ref[at * cells : (at + 1) * cells, :].astype(F32)
-            far = far_ref[at * cells : (at + 1) * cells, :].astype(F32)
-            if r < HALO:
-                total = total + either(place_ref[1], far, near)
-            else:
-                total = total + either(place_ref[1], near, far)
-        out_ref[:, r, :] = state_ref[:, r, :] + step * jnp.transpose(total) + spread * noise_ref[:, r, :]
-
-
-def final_pass(place, step, own, near, far, state, noise):
+    )(level, step, *in_hbm(pulled, *strips, pre, *slopes, *weights, state, noise))
+
+
+def final_kernel(place_ref, step_ref, base_ref, near_ref, far_ref, out_ref):
+    rows = base_ref.shape[1]
+    step = jnp.full((1, 128), step_ref[0], F32)
+    out_ref[...] = base_ref[...]
+    for i in range(HALO):
+        near = near_ref[i].astype(F32)
+        far = far_ref[i].astype(F32)
+        r = rows - HALO + i
+        out_ref[:, i, :] = base_ref[:, i, :] + step * either(place_ref[1], far, near)
+        out_ref[:, r, :] = base_ref[:, r, :] + step * either(place_ref[1], near, far)
+
+
+def final_pass(place, step, base, near, far):
     return pl.pallas_call(
         final_kernel,
-        out_shape=jax.ShapeDtypeStruct(state.shape, F32),
-        in_specs=[smem_spec()] + vmem_specs(6),
+        out_shape=jax.ShapeDtypeStruct(base.shape, F32),
+        in_specs=[smem_spec(), smem_spec()] + vmem_specs(3),
         out_specs=vmem_specs(1)[0],
-        compiler_params=params(16),
+        compiler_params=params(8),
         name="final_pass",
-    )(place, step, *in_hbm(own), near, far, *near_core(state, noise))
+    )(place, step, base, near, far)
 
 
 def swap_pairs(size, first, wrap):
@@ -657,9 +678,9 @@
 
     holders = lax.axis_size(("lon", "lat"))
     packed = pack_blocks(obs_holder, obs_tile, obs_values, holders * CAPACITY, bands * CAPACITY)
-    own, *edges = turn_state(place, state)
+    own, outer, *edges = turn_state(place, state)
     lon_halo = swap("lon", True, *edges)
-    framed = frame_rows(place, own, *lon_halo, width)
+    framed = frame_rows(place, outer, *lon_halo, width)
     packed, framed = lax.optimization_barrier((packed, framed))
     lat_halo = swap("lat", False, *framed)
     recv = lax.all_to_all(
@@ -674,8 +695,8 @@
         place, recv, pred, pred_edge, slopes, operator, precision, precision_edge, weights, channels
     )
     near, far = swap("lat", False, near, far)
-    own = inner_pass(noise_level.reshape(1, 1), pulled, strips, pre, slopes, weights)
-    return final_pass(place, step_size.reshape(1, 1), own, near, far, state, noise)
+    base = inner_pass(noise_level, step_size, pulled, strips, pre, slopes, weights, state, noise)
+    return final_pass(place, step_size, base, near, far)
 
 
 def solution(mesh):

time: 119 us -> 116 us (0.975)
  local copies, waits for them, and re-layouts: 2.89 us -> 0.22 us
    unnamed x16 -> x4, local copies, waits for them, and re-layouts: 2.68 us -> 0.01 us
    pallas_call x2, Pallas kernels: 21.6 us -> 19.4 us  [the longest x1 17 us: inner_pass(): pl.pallas_call(inner_kernel, out_shape=jax.ShapeDtypeStruct(state.shape,...]
    pallas_call x1, Pallas kernels: 2.31 us -> 3.55 us  [turn_state(): pl.pallas_call(turn_kernel, out_shape=(pltpu.HBM((rows * cells, channels)...]
  transfers between devices with their start and end apart: 7 -> 7, of which waited for: 1 -> 1; matrix products, arithmetic and copies ran while one was open for 0% -> 0% of each run, Pallas kernels for 36% -> 38%
where the time goes in v3:
time: 116 us
  Pallas kernels  62.6 us (54%)
  waiting for transfers between devices  26.7 us (23%)
  starting transfers between devices  24.6 us (21%)
  between operations  1.44 us (1%)
    ppermute x3, waiting for transfers between devices, swap(): lax.ppermute(near, axis, swap_pairs(size, 0, wrap))  26.7 us
    pallas_call x1, Pallas kernels, forward_pass(): pl.pallas_call(forward_kernel, out_shape=(pltpu.HBM(pre, F32), pltpu.HBM(...  23.4 us
    pallas_call x1, Pallas kernels, inner_pass(): pl.pallas_call(inner_kernel, out_shape=jax.ShapeDtypeStruct(state.shape,...  17 us
    ppermute x3, starting transfers between devices, swap(): lax.ppermute(far, axis, swap_pairs(size, 1, wrap))  13.8 us
    pallas_call x1, Pallas kernels, edge_pass(): pl.pallas_call(edge_kernel, out_shape=(pltpu.HBM((rows, width, channels),...  12 us
    all_to_all x1, starting transfers between devices, shards(): lax.all_to_all(packed.reshape(holders, CAPACITY * SLOT, cells), ('lon', '...  7.55 us
    pallas_call x1, Pallas kernels, turn_state(): pl.pallas_call(turn_kernel, out_shape=(pltpu.HBM((rows * cells, channels)...  3.55 us
    pallas_call x1, Pallas kernels, pack_blocks(): pl.pallas_call(functools.partial(pack_kernel, shift=shift), out_shape=jax...  3.49 us
  transfers between devices with their start and end apart: 7, of which 1 were waited for; matrix products, arithmetic and copies ran while one was open for 0% of the time, Pallas kernels for 38%

profile of v3, /device:TPU:6, one launch (start us, length us, event | category | flops | bytes accessed | tf_op | source)
XLA Modules:
  0.0 115.7 jit_solution(9523892307521251978)
XLA Ops:
  0.0 0.1 add_convert_fusion.place_ref
  0.1 3.6 %turn_state.1 = (bf16[2048,168]{1,0:T(8,128)(2,1)}, bf16[1024,168]{1,0:T(8,128)(2,1)S(1)}, bf16[128,168]{1,0:T(8,128)(2,1)S(1)}, bf16[128,168]{1,0:T(8,128)(2,1)S(1)}) custom-call(s32[4]{0:T(128)S(1)} %add_convert_fusion.place_ref, f32[168,16,128]{2,1,0:T(8,128)} %state_far.3), custom_call_target="tpu_custom_call" | custom-call | tf_op jit(solution)/shard_map/turn_state/pallas_call | solution.py:205
  3.6 0.1 collective-permute-start
  3.7 5.2 %collective-permute-start.1 = (bf16[128,168]{1,0:T(8,128)(2,1)S(1)}, bf16[128,168]{1,0:T(8,128)(2,1)S(1)}, u32[]{:S(2)}, u32[]{:S(2)}) collective-permute-start(bf16[128,168]{1,0:T(8,128)(2,1)S(1)} %get-tuple-element.28), channel_id=1, source_target_pairs={{8,16},{16,8},{24,32},{32,24},{40,48},{48,40},{56,64},{64,56},{72,... | collective-permute-start | bytes 129032 | tf_op jit(solution)/shard_map/ppermute | solution.py:651
  8.9 3.5 %pack_blocks.1 = bf16[6144,128]{1,0:T(8,128)(2,1)} custom-call(s32[1,96]{1,0:T(1,128)} %bitcast.17, s32[1,96]{1,0:T(1,128)} %bitcast.18, bf16[22,96,128]{2,1,0:T(8,128)(2,1)} %bitcast.15), custom_call_target="tpu_custom_call" | custom-call | tf_op jit(solution)/shard_map/pack_blocks/pallas_call | solution.py:92
  12.4 0.0 collective-permute-done.lon_near_ref
  12.4 0.0 collective-permute-done.1.lon_far_ref
  12.4 0.7 frame_rows.1
  13.1 0.0 copy-start.1
  13.1 0.0 copy-start
  13.1 7.6 %all-to-all-start = ((bf16[128,48,128]{2,1,0:T(8,128)(2,1)}), bf16[128,48,128]{2,1,0:T(8,128)(2,1)S(1)}, u32[]{:S(2)}, u32[]{:S(2)}) async-start(bf16[128,48,128]{2,1,0:T(8,128)(2,1)} %bitcast.7), calls=%async_computation | async-start | bytes 3145728 | tf_op jit(solution)/shard_map/all_to_all | solution.py:686
  20.6 3.1 %collective-permute-start.2 = (bf16[576,168]{1,0:T(8,128)(2,1)S(1)}, bf16[576,168]{1,0:T(8,128)(2,1)S(1)}, u32[]{:S(2)}, u32[]{:S(2)}) collective-permute-start(bf16[576,168]{1,0:T(8,128)(2,1)S(1)} %get-tuple-element.33), channel_id=1, source_target_pairs={{0,1},{1,0},{2,3},{3,2},{4,5},{5,4},{6,7},{7,6},{8,9},{9,8},{10,11... | collective-permute-start | bytes 580616 | tf_op jit(solution)/shard_map/ppermute | solution.py:651
  23.7 2.7 %collective-permute-start.3 = (bf16[576,168]{1,0:T(8,128)(2,1)S(1)}, bf16[576,168]{1,0:T(8,128)(2,1)S(1)}, u32[]{:S(2)}, u32[]{:S(2)}) collective-permute-start(bf16[576,168]{1,0:T(8,128)(2,1)S(1)} %get-tuple-element.34), channel_id=1, source_target_pairs={{1,2},{2,1},{3,4},{4,3},{5,6},{6,5},{9,10},{10,9},{11,12},{12,11},... | collective-permute-start | bytes 580616 | tf_op jit(solution)/shard_map/ppermute | solution.py:651
  26.5 0.0 copy-done.1
  26.5 0.1 copy.13
  26.6 0.1 broadcast_in_dim_tile.3
  26.7 0.0 copy-done
  26.7 26.7 %collective-permute-done.2.lat_near_ref = bf16[576,168]{1,0:T(8,128)(2,1)S(1)} collective-permute-done((bf16[576,168]{1,0:T(8,128)(2,1)S(1)}, bf16[576,168]{1,0:T(8,128)(2,1)S(1)}, u32[]{:S(2)}, u32[]{:S(2)}) %collective-permute-start.2) | collective-permute-done | bytes 193568 | tf_op jit(solution)/shard_map/ppermute | solution.py:651
  53.4 0.0 collective-permute-done.3.lat_far_ref
  53.4 23.4 %forward_pass.1 = (f32[16,144,168]{2,1,0:T(8,128)}, f32[16,32,128]{2,1,0:T(8,128)}, f32[2,16,128]{2,1,0:T(8,128)}, bf16[3168,256]{1,0:T(8,128)(2,1)}, bf16[2880,...) custom-call(s32[4]{0:T(128)S(1)} %add_convert_fusion.place_ref, bf16[2048,168]{1,0:T(8,128)(2,1)} %get-tuple-element.32.own_ref, ...), custom_call_target="tpu_custom_call" | custom-call | tf_op jit(solution)/shard_map/forward_pass/pallas_call | solution.py:363
  76.9 0.0 all-to-all-done
  76.9 12.0 %edge_pass.1 = (f32[16,144,168]{2,1,0:T(8,128)}, bf16[4,168,128]{2,1,0:T(8,128)(2,1)S(1)}, bf16[4,168,128]{2,1,0:T(8,128)(2,1)S(1)}, bf16[576,256]{1,0:T(8,128)(...) custom-call(s32[4]{0:T(128)S(1)} %add_convert_fusion.place_ref, bf16[6144,128]{1,0:T(8,128)(2,1)S(1)} %bitcast.11, ...), custom_call_target="tpu_custom_call" | custom-call | tf_op jit(solution)/shard_map/edge_pass/pallas_call | solution.py:502
  88.9 0.1 collective-permute-start.4
  89.0 6.0 %collective-permute-start.5 = (bf16[4,168,128]{2,1,0:T(8,128)(2,1)S(1)}, bf16[4,168,128]{2,1,0:T(8,128)(2,1)S(1)}, u32[]{:S(2)}, u32[]{:S(2)}) collective-permute-start(bf16[4,168,128]{2,1,0:T(8,128)(2,1)S(1)} %get-tuple-element.46), channel_id=1, source_target_pairs={{1,2},{2,1},{3,4},{4,3},{5,6},{6,5},{9,10},{10,9},{11,12},{12,11},... | collective-permute-start | bytes 516104 | tf_op jit(solution)/shard_map/ppermute | solution.py:651
  96.2 17.0 %inner_pass.1.base_ref = f32[168,16,128]{2,1,0:T(8,128)S(1)} custom-call(f32[1]{0:T(128)S(6)} %copy.14.level_ref, f32[1]{0:T(128)S(6)} %copy.15.step_ref, f32[16,144,168]{2,1,0:T(8,128)} %get-tuple-element.40.pulled_ref, bf16[576,256]{1,0:T(8,128)(2,1)} %get-tuple-element.41.s0_ref, bf16[576,256]{1,0:T(8,128)(2,1)} %get-tuple-element.42.s1_ref, ...), custom_call_target="tpu_custom_call" | custom-call | tf_op jit(solution)/shard_map/inner_pass/pallas_call | solution.py:601
  113.2 0.0 collective-permute-done.4.near_ref
  113.2 0.0 collective-permute-done.5.far_ref
  113.2 2.4 %final_pass.1 = f32[168,16,128]{2,1,0:T(8,128)} custom-call(s32[4]{0:T(128)S(1)} %add_convert_fusion.place_ref, f32[1]{0:T(128)S(6)} %copy.15.step_ref, f32[168,16,128]{2,1,0:T(8,128)S(1)} %inner_pass.1.base_ref, bf16[4,168,128]{2,1,0:T(8,128)(2,1)S(1)} %collective-permute-done.4.near_ref, bf16[4,168,128]{2,1,0:T(8,128)(2,1)S(1)} %collective-permute-done.5.far_ref), custom_call_target="tpu_custom_call" | custom-call | tf_op jit(solution)/shard_map/final_pass/pallas_call | solution.py:631
  (5 shorter events, 0.0 us)
Async XLA Ops:
  3.6 8.7 %collective-permute-start = (bf16[128,168]{1,0:T(8,128)(2,1)S(1)}, bf16[128,168]{1,0:T(8,128)(2,1)S(1)}, u32[]{:S(2)}, u32[]{:S(2)}) collective-permute-start(bf16[128,168]{1,0:T(8,128)(2,1)S(1)} %get-tuple-element.27), channel_id=1, source_target_pairs={{0,8},{8,0},{16,24},{24,16},{32,40},{40,32},{48,56},{56,48},{64,72... | collective-permute-start | bytes 129032 | tf_op jit(solution)/shard_map/ppermute | solution.py:651
  3.7 8.6 %collective-permute-start.1 = (bf16[128,168]{1,0:T(8,128)(2,1)S(1)}, bf16[128,168]{1,0:T(8,128)(2,1)S(1)}, u32[]{:S(2)}, u32[]{:S(2)}) collective-permute-start(bf16[128,168]{1,0:T(8,128)(2,1)S(1)} %get-tuple-element.28), channel_id=1, source_target_pairs={{8,16},{16,8},{24,32},{32,24},{40,48},{48,40},{56,64},{64,56},{72,... | collective-permute-start | bytes 129032 | tf_op jit(solution)/shard_map/ppermute | solution.py:651
  13.1 13.4 %copy-start.1 = (f32[22]{0:T(128)S(1)}, f32[22]{0:T(128)}, u32[]{:S(2)}) copy-start(f32[22]{0:T(128)} %param.21) | copy-start | bytes 268
  13.1 13.6 %copy-start = (bf16[22,168]{1,0:T(8,128)(2,1)S(1)}, bf16[22,168]{1,0:T(8,128)(2,1)}, u32[]{:S(2)}) copy-start(bf16[22,168]{1,0:T(8,128)(2,1)} %param.20) | copy-start | bytes 22180
  13.1 63.8 %all-to-all-start = ((bf16[128,48,128]{2,1,0:T(8,128)(2,1)}), bf16[128,48,128]{2,1,0:T(8,128)(2,1)S(1)}, u32[]{:S(2)}, u32[]{:S(2)}) async-start(bf16[128,48,128]{2,1,0:T(8,128)(2,1)} %bitcast.7), calls=%async_computation | async-start | bytes 3145728 | tf_op jit(solution)/shard_map/all_to_all | solution.py:686
  20.6 32.8 %collective-permute-start.2 = (bf16[576,168]{1,0:T(8,128)(2,1)S(1)}, bf16[576,168]{1,0:T(8,128)(2,1)S(1)}, u32[]{:S(2)}, u32[]{:S(2)}) collective-permute-start(bf16[576,168]{1,0:T(8,128)(2,1)S(1)} %get-tuple-element.33), channel_id=1, source_target_pairs={{0,1},{1,0},{2,3},{3,2},{4,5},{5,4},{6,7},{7,6},{8,9},{9,8},{10,11... | collective-permute-start | bytes 580616 | tf_op jit(solution)/shard_map/ppermute | solution.py:651
  23.7 29.7 %collective-permute-start.3 = (bf16[576,168]{1,0:T(8,128)(2,1)S(1)}, bf16[576,168]{1,0:T(8,128)(2,1)S(1)}, u32[]{:S(2)}, u32[]{:S(2)}) collective-permute-start(bf16[576,168]{1,0:T(8,128)(2,1)S(1)} %get-tuple-element.34), channel_id=1, source_target_pairs={{1,2},{2,1},{3,4},{4,3},{5,6},{6,5},{9,10},{10,9},{11,12},{12,11},... | collective-permute-start | bytes 580616 | tf_op jit(solution)/shard_map/ppermute | solution.py:651
  88.9 24.3 %collective-permute-start.4 = (bf16[4,168,128]{2,1,0:T(8,128)(2,1)S(1)}, bf16[4,168,128]{2,1,0:T(8,128)(2,1)S(1)}, u32[]{:S(2)}, u32[]{:S(2)}) collective-permute-start(bf16[4,168,128]{2,1,0:T(8,128)(2,1)S(1)} %get-tuple-element.45), channel_id=1, source_target_pairs={{0,1},{1,0},{2,3},{3,2},{4,5},{5,4},{6,7},{7,6},{8,9},{9,8},{10,11... | collective-permute-start | bytes 516104 | tf_op jit(solution)/shard_map/ppermute | solution.py:651
  89.0 24.2 %collective-permute-start.5 = (bf16[4,168,128]{2,1,0:T(8,128)(2,1)S(1)}, bf16[4,168,128]{2,1,0:T(8,128)(2,1)S(1)}, u32[]{:S(2)}, u32[]{:S(2)}) collective-permute-start(bf16[4,168,128]{2,1,0:T(8,128)(2,1)S(1)} %get-tuple-element.46), channel_id=1, source_target_pairs={{1,2},{2,1},{3,4},{4,3},{5,6},{6,5},{9,10},{10,9},{11,12},{12,11},... | collective-permute-start | bytes 516104 | tf_op jit(solution)/shard_map/ppermute | solution.py:651

commit v4 on v3

--- a/solution.py
+++ b/solution.py
@@ -84,7 +84,7 @@
     at = lax.broadcasted_iota(jnp.int32, (slots, width), 1)
     wide_ref[pl.ds(BANDS, slots, stride=SLOT), :] = jnp.where(at == BANDS + 1, own, before)
     wide_ref[pl.ds(BANDS + 1, slots, stride=SLOT), :] = after
-    out_ref[...] = wide_ref[...].astype(BF16)
+    out_ref[...] = wide_ref[0 : slots * SLOT, :].astype(BF16)
 
 
 def pack_blocks(holders, tiles, values, slot_count, shift):
@@ -94,7 +94,7 @@
         out_shape=jax.ShapeDtypeStruct((slot_count * SLOT, width), BF16),
         in_specs=vmem_specs(3),
         out_specs=vmem_specs(1)[0],
-        scratch_shapes=[pltpu.VMEM((slot_count * SLOT, width), F32)],
+        scratch_shapes=[pltpu.VMEM(((slot_count + 1) * SLOT, width), F32)],
         compiler_params=params(12),
         name="pack_blocks",
     )(*in_hbm(holders.reshape(1, -1), tiles.reshape(1, -1), jnp.transpose(values, (1, 0, 2))))
@@ -270,7 +270,7 @@
     loads = copies(
         ((w0_far, w0), (wm_far.at[0], wm.at[0]), (wm_far.at[1], wm.at[1]), (w3_far, w3)), in_sems
     )
-    stores = copies(((d0, d0_far), (d1, d1_far), (d2, d2_far), (pre_ref, pre_far)), out_sems)
+    stores = copies(((d0, d0_far), (d1, d1_far), (d2, d2_far)), out_sems)
     for load in loads:
         load.start()
 
@@ -321,6 +321,12 @@
                         (((1,), (1,)), ((), ())),
                         preferred_element_type=F32,
                     )
+                at = pl.ds(row, n)
+                store = pltpu.make_async_copy(
+                    pre_ref.at[at], pre_far.at[at], out_sems.at[LAYERS - 1 + row // BLOCK]
+                )
+                store.start()
+                stores.append(store)
 
         conv_layer(count, compute, finish, acc_a, acc_b)
         if layer < LAYERS - 1:
@@ -338,7 +344,8 @@
             def _(count=count, size=size):
                 clear(count * width - size)
 
-        stores[layer].start()
+        if layer < LAYERS - 1:
+            stores[layer].start()
         src, dst = dst, src
     tall = jnp.concatenate([op_ref[:, 0:channels].astype(F32), jnp.zeros((96, channels), F32)], axis=0).astype(BF16)
     for end, first in ((0, SIDE - EDGE), (1, SIDE + cells)):
@@ -373,9 +380,9 @@
         scratch_shapes=[pltpu.VMEM((padded, 3 * LANES), BF16)] * 2
         + [pltpu.VMEM((BLOCK * width, LANES), F32)] * 2
         + weight_scratch(weights)
-        + [pltpu.VMEM(pre, F32)] + [pltpu.VMEM((rows * width, 128), F32)] * 2
+        + [pltpu.VMEM(pre, F32)] + [pltpu.VMEM(((rows + 1) * width, 128), F32)] * 2
         + [pltpu.VMEM(shape, BF16) for shape in slopes]
-        + [pltpu.SemaphoreType.DMA((LAYERS,)), pltpu.SemaphoreType.DMA((LAYERS,))],
+        + [pltpu.SemaphoreType.DMA((LAYERS,)), pltpu.SemaphoreType.DMA((LAYERS - 1 + rows // BLOCK,))],
         compiler_params=params(34),
         name="forward_pass",
     )(place, *in_hbm(own), *lon, *lat, operator, *in_hbm(*weights))
@@ -391,8 +398,8 @@
 def edge_kernel(
     place_ref, recv_ref, pred_ref, pred_edge_ref, op_ref, prec_ref, prec_edge_ref,
     d0_far, d1_far, d2_far, w0_far, wm_far, w3_far,
-    pulled_ref, near_ref, far_ref, s0_ref, s1_ref, s2_ref,
-    wide_ref, sums_ref, field_a, field_b, buf_a, buf_b, acc_a, acc_b, w0, wm, w3, d_ref, in_sems,
+    pulled_far, near_ref, far_ref, s0_ref, s1_ref, s2_ref,
+    pulled_ref, pulled_sem, wide_ref, sums_ref, field_a, field_b, buf_a, buf_b, acc_a, acc_b, w0, wm, w3, d_ref, in_sems,
 ):
     rows, cells, channels = pred_ref.shape[0], pred_ref.shape[2], near_ref.shape[1]
     width = cells + 2 * SIDE
@@ -416,7 +423,7 @@
     buf_b[0 : 4 * width, :] = nothing
     buf_b[(rows + 6) * width : (rows + 10) * width, :] = nothing
 
-    wide_ref[...] = recv_ref[...].astype(F32)
+    wide_ref[0 : slots * SLOT, :] = recv_ref[...].astype(F32)
     sums_ref[...] = jnp.zeros(sums_ref.shape, F32)
     sides = [wide_ref[pl.ds(BANDS + end, slots, stride=SLOT), :] for end in range(2)]
     lane = lax.broadcasted_iota(jnp.int32, (slots, cells), 1).astype(F32)
@@ -464,6 +471,8 @@
         pulled_ref[r] = row
         if r < HALO or r >= rows - HALO:
             put_shifted(buf_a, r + LEAD, width, row)
+    sent = copies(((pulled_ref, pulled_far),), pulled_sem)[0]
+    sent.start()
 
     src, dst = buf_a, buf_b
     for layer in range(LAYERS - 1, -1, -1):
@@ -492,6 +501,7 @@
                 near_ref[i] = jnp.transpose(either(place_ref[1], low, top)).astype(BF16)
                 far_ref[i] = jnp.transpose(either(place_ref[1], top, low)).astype(BF16)
         src, dst = dst, src
+    sent.wait()
 
 
 def edge_pass(place, recv, pred, pred_edge, slopes, operator, precision, precision_edge, weights, channels):
@@ -508,12 +518,14 @@
         )
         + tuple(pltpu.HBM((size, LANES), BF16) for _ in range(LAYERS - 1)),
         in_specs=[smem_spec()] + vmem_specs(6) + far_specs(6),
-        out_specs=tuple(vmem_specs(6)),
+        out_specs=tuple(far_specs(1) + vmem_specs(5)),
         scratch_shapes=[
-            pltpu.VMEM(recv.shape, F32),
-            pltpu.VMEM((rows * 32, recv.shape[1]), F32),
-            pltpu.VMEM((rows * width, 128), F32),
-            pltpu.VMEM((rows * width, 128), F32),
+            pltpu.VMEM((rows, width, channels), F32),
+            pltpu.SemaphoreType.DMA((1,)),
+            pltpu.VMEM((recv.shape[0] + SLOT, recv.shape[1]), F32),
+            pltpu.VMEM(((rows + 1) * 32, recv.shape[1]), F32),
+            pltpu.VMEM(((rows + 1) * width, 128), F32),
+            pltpu.VMEM(((rows + 1) * width, 128), F32),
         ]
         + [pltpu.VMEM((padded, 3 * LANES), BF16)] * 2
         + [pltpu.VMEM((size, LANES), F32)] * 2
@@ -525,16 +537,16 @@
 
 
 def inner_kernel(
-    level_ref, step_ref, pulled_ref, s0_ref, s1_ref, s2_ref,
+    scale_ref, pulled_ref, s0_ref, s1_ref, s2_ref,
     pre_far, d0_far, d1_far, d2_far, w0_far, wm_far, w3_far, state_far, noise_far,
     base_ref,
     buf_a, buf_b, acc_a, acc_b, w0, wm, w3, pre_ref, d0, d1, d2, state_ref, noise_ref, in_sems,
 ):
     rows, width, _ = pulled_ref.shape
     cells = width - 2 * SIDE
-    level = jnp.full((1, 128), level_ref[0], F32)
+    level = jnp.full((1, 128), scale_ref[0], F32)
     inverse = (1.0 / (level * level))[:, 0:1]
-    step = jnp.full((1, 128), step_ref[0], F32)
+    step = jnp.full((1, 128), scale_ref[1], F32)
     spread = jnp.sqrt(2.0 * step)
     weights = (w0, wm.at[0], wm.at[1], w3)
     strips = (s0_ref, s1_ref, s2_ref)
@@ -554,7 +566,7 @@
         put_shifted(buf_a, r + LEAD, width, pulled_ref[r])
         return carry
 
-    lax.fori_loop(0, rows, fill, 0)
+    lax.fori_loop(LAYERS - 2, rows - LAYERS + 2, fill, 0)
     loads[0].wait()
     src, dst = buf_a, buf_b
     half = HALO // 2 * width
@@ -594,14 +606,14 @@
         src, dst = dst, src
 
 
-def inner_pass(level, step, pulled, strips, pre, slopes, weights, state, noise):
+def inner_pass(scale, pulled, strips, pre, slopes, weights, state, noise):
     rows, width, _ = pre.shape
     padded = (rows + 2 * LEAD) * width
     kept = [((rows - 2 * (layer + 1)) * width, LANES) for layer in range(LAYERS - 1)]
     return pl.pallas_call(
         inner_kernel,
         out_shape=jax.ShapeDtypeStruct(state.shape, F32),
-        in_specs=[smem_spec(), smem_spec()] + vmem_specs(4) + far_specs(9),
+        in_specs=[smem_spec()] + vmem_specs(4) + far_specs(9),
         out_specs=vmem_specs(1)[0],
         scratch_shapes=[pltpu.VMEM((padded, 3 * LANES), BF16)] * 2
         + [pltpu.VMEM((BLOCK * width, LANES), F32)] * 2
@@ -612,12 +624,12 @@
         + [pltpu.SemaphoreType.DMA((2 * LAYERS + 2,))],
         compiler_params=params(34),
         name="inner_pass",
-    )(level, step, *in_hbm(pulled, *strips, pre, *slopes, *weights, state, noise))
-
-
-def final_kernel(place_ref, step_ref, base_ref, near_ref, far_ref, out_ref):
+    )(scale, *in_hbm(pulled, *strips, pre, *slopes, *weights, state, noise))
+
+
+def final_kernel(place_ref, scale_ref, base_ref, near_ref, far_ref, out_ref):
     rows = base_ref.shape[1]
-    step = jnp.full((1, 128), step_ref[0], F32)
+    step = jnp.full((1, 128), scale_ref[1], F32)
     out_ref[...] = base_ref[...]
     for i in range(HALO):
         near = near_ref[i].astype(F32)
@@ -627,7 +639,7 @@
         out_ref[:, r, :] = base_ref[:, r, :] + step * either(place_ref[1], near, far)
 
 
-def final_pass(place, step, base, near, far):
+def final_pass(place, scale, base, near, far):
     return pl.pallas_call(
         final_kernel,
         out_shape=jax.ShapeDtypeStruct(base.shape, F32),
@@ -635,7 +647,7 @@
         out_specs=vmem_specs(1)[0],
         compiler_params=params(8),
         name="final_pass",
-    )(place, step, base, near, far)
+    )(place, scale, base, near, far)
 
 
 def swap_pairs(size, first, wrap):
@@ -695,8 +707,9 @@
         place, recv, pred, pred_edge, slopes, operator, precision, precision_edge, weights, channels
     )
     near, far = swap("lat", False, near, far)
-    base = inner_pass(noise_level, step_size, pulled, strips, pre, slopes, weights, state, noise)
-    return final_pass(place, step_size, base, near, far)
+    scale = jnp.concatenate([noise_level, step_size])
+    base = inner_pass(scale, pulled, strips, pre, slopes, weights, state, noise)
+    return final_pass(place, scale, base, near, far)
 
 
 def solution(mesh):
@@ -715,6 +728,4 @@
         P(),
     )
 
-    return jax.shard_map(
-        shards, mesh=mesh, in_specs=placed, out_specs=P(None, "lat", "lon"), check_vma=False
-    )
+    return jax.shard_map(shards, mesh=mesh, in_specs=placed, out_specs=P(None, "lat", "lon"), check_vma=False)

time: 116 us -> 116 us (level)
  no operation moved by 1% of the time
where the time goes in v4:
time: 116 us; the launch traced here: 115 us
  Pallas kernels  62.3 us (54%)
  waiting for transfers between devices  26.7 us (23%)
  starting transfers between devices  24.6 us (21%)
  between operations  1.44 us (1%)
    ppermute x3, waiting for transfers between devices, swap(): lax.ppermute(near, axis, swap_pairs(size, 0, wrap))  26.7 us
    pallas_call x1, Pallas kernels, forward_pass(): pl.pallas_call(forward_kernel, out_shape=(pltpu.HBM(pre, F32), pltpu.HBM(...  23 us
    pallas_call x1, Pallas kernels, inner_pass(): pl.pallas_call(inner_kernel, out_shape=jax.ShapeDtypeStruct(state.shape,...  17 us
    ppermute x3, starting transfers between devices, swap(): lax.ppermute(far, axis, swap_pairs(size, 1, wrap))  13.8 us
    pallas_call x1, Pallas kernels, edge_pass(): pl.pallas_call(edge_kernel, out_shape=(pltpu.HBM((rows, width, channels),...  12.1 us
    all_to_all x1, starting transfers between devices, shards(): lax.all_to_all(packed.reshape(holders, CAPACITY * SLOT, cells), ('lon', '...  7.55 us
    pallas_call x1, Pallas kernels, turn_state(): pl.pallas_call(turn_kernel, out_shape=(pltpu.HBM((rows * cells, channels)...  3.55 us
    pallas_call x1, Pallas kernels, pack_blocks(): pl.pallas_call(functools.partial(pack_kernel, shift=shift), out_shape=jax...  3.49 us
  transfers between devices with their start and end apart: 7, of which 1 were waited for; matrix products, arithmetic and copies ran while one was open for 0% of the time, Pallas kernels for 38%

profile of v4, /device:TPU:6, one launch (start us, length us, event | category | flops | bytes accessed | tf_op | source)
XLA Modules:
  0.0 115.5 jit_solution(8823682746326648873)
XLA Ops:
  0.0 0.1 add_convert_fusion.place_ref
  0.1 3.6 %turn_state.1 = (bf16[2048,168]{1,0:T(8,128)(2,1)}, bf16[1024,168]{1,0:T(8,128)(2,1)S(1)}, bf16[128,168]{1,0:T(8,128)(2,1)S(1)}, bf16[128,168]{1,0:T(8,128)(2,1)S(1)}) custom-call(s32[4]{0:T(128)S(1)} %add_convert_fusion.place_ref, f32[168,16,128]{2,1,0:T(8,128)} %state_far.3), custom_call_target="tpu_custom_call" | custom-call | tf_op jit(solution)/shard_map/turn_state/pallas_call | solution.py:205
  3.6 0.1 collective-permute-start
  3.7 5.2 %collective-permute-start.1 = (bf16[128,168]{1,0:T(8,128)(2,1)S(1)}, bf16[128,168]{1,0:T(8,128)(2,1)S(1)}, u32[]{:S(2)}, u32[]{:S(2)}) collective-permute-start(bf16[128,168]{1,0:T(8,128)(2,1)S(1)} %get-tuple-element.28), channel_id=1, source_target_pairs={{8,16},{16,8},{24,32},{32,24},{40,48},{48,40},{56,64},{64,56},{72,... | collective-permute-start | bytes 129032 | tf_op jit(solution)/shard_map/ppermute | solution.py:663
  8.9 3.5 %pack_blocks.1 = bf16[6144,128]{1,0:T(8,128)(2,1)} custom-call(s32[1,96]{1,0:T(1,128)} %bitcast.17, s32[1,96]{1,0:T(1,128)} %bitcast.18, bf16[22,96,128]{2,1,0:T(8,128)(2,1)} %bitcast.15), custom_call_target="tpu_custom_call" | custom-call | tf_op jit(solution)/shard_map/pack_blocks/pallas_call | solution.py:92
  12.4 0.0 collective-permute-done.lon_near_ref
  12.4 0.0 collective-permute-done.1.lon_far_ref
  12.4 0.7 frame_rows.1
  13.1 0.0 copy-start.1
  13.1 0.0 copy-start
  13.1 7.6 %all-to-all-start = ((bf16[128,48,128]{2,1,0:T(8,128)(2,1)}), bf16[128,48,128]{2,1,0:T(8,128)(2,1)S(1)}, u32[]{:S(2)}, u32[]{:S(2)}) async-start(bf16[128,48,128]{2,1,0:T(8,128)(2,1)} %bitcast.7), calls=%async_computation | async-start | bytes 3145728 | tf_op jit(solution)/shard_map/all_to_all | solution.py:698
  20.6 3.1 %collective-permute-start.2 = (bf16[576,168]{1,0:T(8,128)(2,1)S(1)}, bf16[576,168]{1,0:T(8,128)(2,1)S(1)}, u32[]{:S(2)}, u32[]{:S(2)}) collective-permute-start(bf16[576,168]{1,0:T(8,128)(2,1)S(1)} %get-tuple-element.33), channel_id=1, source_target_pairs={{0,1},{1,0},{2,3},{3,2},{4,5},{5,4},{6,7},{7,6},{8,9},{9,8},{10,11... | collective-permute-start | bytes 580616 | tf_op jit(solution)/shard_map/ppermute | solution.py:663
  23.7 2.7 %collective-permute-start.3 = (bf16[576,168]{1,0:T(8,128)(2,1)S(1)}, bf16[576,168]{1,0:T(8,128)(2,1)S(1)}, u32[]{:S(2)}, u32[]{:S(2)}) collective-permute-start(bf16[576,168]{1,0:T(8,128)(2,1)S(1)} %get-tuple-element.34), channel_id=1, source_target_pairs={{1,2},{2,1},{3,4},{4,3},{5,6},{6,5},{9,10},{10,9},{11,12},{12,11},... | collective-permute-start | bytes 580616 | tf_op jit(solution)/shard_map/ppermute | solution.py:663
  26.5 0.0 copy-done.1
  26.5 0.1 copy.13
  26.6 0.1 broadcast_in_dim_tile.3
  26.7 0.0 copy-done
  26.7 26.7 %collective-permute-done.2.lat_near_ref = bf16[576,168]{1,0:T(8,128)(2,1)S(1)} collective-permute-done((bf16[576,168]{1,0:T(8,128)(2,1)S(1)}, bf16[576,168]{1,0:T(8,128)(2,1)S(1)}, u32[]{:S(2)}, u32[]{:S(2)}) %collective-permute-start.2) | collective-permute-done | bytes 193568 | tf_op jit(solution)/shard_map/ppermute | solution.py:663
  53.4 0.0 collective-permute-done.3.lat_far_ref
  53.4 23.0 %forward_pass.1 = (f32[16,144,168]{2,1,0:T(8,128)}, f32[16,32,128]{2,1,0:T(8,128)}, f32[2,16,128]{2,1,0:T(8,128)}, bf16[3168,256]{1,0:T(8,128)(2,1)}, bf16[2880,...) custom-call(s32[4]{0:T(128)S(1)} %add_convert_fusion.place_ref, bf16[2048,168]{1,0:T(8,128)(2,1)} %get-tuple-element.32.own_ref, ...), custom_call_target="tpu_custom_call" | custom-call | tf_op jit(solution)/shard_map/forward_pass/pallas_call | solution.py:370
  76.5 0.0 all-to-all-done
  76.5 12.1 %edge_pass.1 = (f32[16,144,168]{2,1,0:T(8,128)}, bf16[4,168,128]{2,1,0:T(8,128)(2,1)S(1)}, bf16[4,168,128]{2,1,0:T(8,128)(2,1)S(1)}, bf16[576,256]{1,0:T(8,128)(...) custom-call(s32[4]{0:T(128)S(1)} %add_convert_fusion.place_ref, bf16[6144,128]{1,0:T(8,128)(2,1)S(1)} %bitcast.11, ...), custom_call_target="tpu_custom_call" | custom-call | tf_op jit(solution)/shard_map/edge_pass/pallas_call | solution.py:512
  88.6 0.1 collective-permute-start.4
  88.7 6.0 %collective-permute-start.5 = (bf16[4,168,128]{2,1,0:T(8,128)(2,1)S(1)}, bf16[4,168,128]{2,1,0:T(8,128)(2,1)S(1)}, u32[]{:S(2)}, u32[]{:S(2)}) collective-permute-start(bf16[4,168,128]{2,1,0:T(8,128)(2,1)S(1)} %get-tuple-element.46), channel_id=1, source_target_pairs={{1,2},{2,1},{3,4},{4,3},{5,6},{6,5},{9,10},{10,9},{11,12},{12,11},... | collective-permute-start | bytes 516104 | tf_op jit(solution)/shard_map/ppermute | solution.py:663
  95.9 0.1 pad_maximum_fusion.scale_ref
  96.0 17.0 %inner_pass.1.base_ref = f32[168,16,128]{2,1,0:T(8,128)S(1)} custom-call(f32[2]{0:T(128)S(1)} %pad_maximum_fusion.scale_ref, f32[16,144,168]{2,1,0:T(8,128)} %get-tuple-element.40.pulled_ref, bf16[576,256]{1,0:T(8,128)(2,1)} %get-tuple-element.41.s0_ref, bf16[576,256]{1,0:T(8,128)(2,1)} %get-tuple-element.42.s1_ref, ...), custom_call_target="tpu_custom_call" | custom-call | tf_op jit(solution)/shard_map/inner_pass/pallas_call | solution.py:613
  113.0 0.0 collective-permute-done.4.near_ref
  113.0 0.0 collective-permute-done.5.far_ref
  113.0 2.5 %final_pass.1 = f32[168,16,128]{2,1,0:T(8,128)} custom-call(s32[4]{0:T(128)S(1)} %add_convert_fusion.place_ref, f32[2]{0:T(128)S(1)} %pad_maximum_fusion.scale_ref, f32[168,16,128]{2,1,0:T(8,128)S(1)} %inner_pass.1.base_ref, bf16[4,168,128]{2,1,0:T(8,128)(2,1)S(1)} %collective-permute-done.4.near_ref, bf16[4,168,128]{2,1,0:T(8,128)(2,1)S(1)} %collective-permute-done.5.far_ref), custom_call_target="tpu_custom_call" | custom-call | tf_op jit(solution)/shard_map/final_pass/pallas_call | solution.py:643
  (5 shorter events, 0.0 us)
Async XLA Ops:
  3.6 8.7 %collective-permute-start = (bf16[128,168]{1,0:T(8,128)(2,1)S(1)}, bf16[128,168]{1,0:T(8,128)(2,1)S(1)}, u32[]{:S(2)}, u32[]{:S(2)}) collective-permute-start(bf16[128,168]{1,0:T(8,128)(2,1)S(1)} %get-tuple-element.27), channel_id=1, source_target_pairs={{0,8},{8,0},{16,24},{24,16},{32,40},{40,32},{48,56},{56,48},{64,72... | collective-permute-start | bytes 129032 | tf_op jit(solution)/shard_map/ppermute | solution.py:663
  3.7 8.6 %collective-permute-start.1 = (bf16[128,168]{1,0:T(8,128)(2,1)S(1)}, bf16[128,168]{1,0:T(8,128)(2,1)S(1)}, u32[]{:S(2)}, u32[]{:S(2)}) collective-permute-start(bf16[128,168]{1,0:T(8,128)(2,1)S(1)} %get-tuple-element.28), channel_id=1, source_target_pairs={{8,16},{16,8},{24,32},{32,24},{40,48},{48,40},{56,64},{64,56},{72,... | collective-permute-start | bytes 129032 | tf_op jit(solution)/shard_map/ppermute | solution.py:663
  13.1 13.4 %copy-start.1 = (f32[22]{0:T(128)S(1)}, f32[22]{0:T(128)}, u32[]{:S(2)}) copy-start(f32[22]{0:T(128)} %param.21) | copy-start | bytes 268
  13.1 13.6 %copy-start = (bf16[22,168]{1,0:T(8,128)(2,1)S(1)}, bf16[22,168]{1,0:T(8,128)(2,1)}, u32[]{:S(2)}) copy-start(bf16[22,168]{1,0:T(8,128)(2,1)} %param.20) | copy-start | bytes 22180
  13.1 63.4 %all-to-all-start = ((bf16[128,48,128]{2,1,0:T(8,128)(2,1)}), bf16[128,48,128]{2,1,0:T(8,128)(2,1)S(1)}, u32[]{:S(2)}, u32[]{:S(2)}) async-start(bf16[128,48,128]{2,1,0:T(8,128)(2,1)} %bitcast.7), calls=%async_computation | async-start | bytes 3145728 | tf_op jit(solution)/shard_map/all_to_all | solution.py:698
  20.6 32.8 %collective-permute-start.2 = (bf16[576,168]{1,0:T(8,128)(2,1)S(1)}, bf16[576,168]{1,0:T(8,128)(2,1)S(1)}, u32[]{:S(2)}, u32[]{:S(2)}) collective-permute-start(bf16[576,168]{1,0:T(8,128)(2,1)S(1)} %get-tuple-element.33), channel_id=1, source_target_pairs={{0,1},{1,0},{2,3},{3,2},{4,5},{5,4},{6,7},{7,6},{8,9},{9,8},{10,11... | collective-permute-start | bytes 580616 | tf_op jit(solution)/shard_map/ppermute | solution.py:663
  23.7 29.7 %collective-permute-start.3 = (bf16[576,168]{1,0:T(8,128)(2,1)S(1)}, bf16[576,168]{1,0:T(8,128)(2,1)S(1)}, u32[]{:S(2)}, u32[]{:S(2)}) collective-permute-start(bf16[576,168]{1,0:T(8,128)(2,1)S(1)} %get-tuple-element.34), channel_id=1, source_target_pairs={{1,2},{2,1},{3,4},{4,3},{5,6},{6,5},{9,10},{10,9},{11,12},{12,11},... | collective-permute-start | bytes 580616 | tf_op jit(solution)/shard_map/ppermute | solution.py:663
  88.6 24.4 %collective-permute-start.4 = (bf16[4,168,128]{2,1,0:T(8,128)(2,1)S(1)}, bf16[4,168,128]{2,1,0:T(8,128)(2,1)S(1)}, u32[]{:S(2)}, u32[]{:S(2)}) collective-permute-start(bf16[4,168,128]{2,1,0:T(8,128)(2,1)S(1)} %get-tuple-element.45), channel_id=1, source_target_pairs={{0,1},{1,0},{2,3},{3,2},{4,5},{5,4},{6,7},{7,6},{8,9},{9,8},{10,11... | collective-permute-start | bytes 516104 | tf_op jit(solution)/shard_map/ppermute | solution.py:663
  88.7 24.3 %collective-permute-start.5 = (bf16[4,168,128]{2,1,0:T(8,128)(2,1)S(1)}, bf16[4,168,128]{2,1,0:T(8,128)(2,1)S(1)}, u32[]{:S(2)}, u32[]{:S(2)}) collective-permute-start(bf16[4,168,128]{2,1,0:T(8,128)(2,1)S(1)} %get-tuple-element.46), channel_id=1, source_target_pairs={{1,2},{2,1},{3,4},{4,3},{5,6},{6,5},{9,10},{10,9},{11,12},{12,11},... | collective-permute-start | bytes 516104 | tf_op jit(solution)/shard_map/ppermute | solution.py:663
